TPU v7x, 128 devices: a whole 4x4x4 slice. The times are simulated.
128 devices in a mesh: group: 8 (over y, x_hi), strip: 16 (over x_lo, z, core).
Axes of the slice: x: 4 (x_hi: 2, x_lo: 2; x = x_hi * 2 + x_lo), y: 4, z: 4, core: 2. Of those that a mesh axis runs over, the one named last changes fastest.
Arguments:
- initial: float32 [8, 512, 1024], P('group', 'strip'), may hold values from -6 to 6
- conductivity: float32 [8, 512, 1024], P('group', 'strip'), may hold values from 0.5 to 1.5
- step_count: int32 [8], P('group'), may hold values from 16 to 32, as said below
- emit_steps: int32 [8, 16], P('group'), may hold values from 1 to 32
- assign: int32 [512], replicated, may hold values from 0 to 127
- sample_inputs: bfloat16 [512, 128], P(('group', 'strip')), may hold values from -6 to 6
- w_first: bfloat16 [128, 512], replicated, may hold values from -0.5 to 0.5
- w_second: bfloat16 [512, 512], replicated, may hold values from -0.25 to 0.25
- w_third: bfloat16 [512, 512], replicated, may hold values from -0.25 to 0.25
- w_out: bfloat16 [512, 512, 1024], P(None, 'strip', 'group'), may hold values from -0.25 to 0.25
Outputs:
- grad_first: float32 [128, 512], replicated
- grad_second: float32 [512, 512], replicated
- grad_third: float32 [512, 512], replicated
- grad_out: bfloat16 [512, 512, 1024], P(None, 'strip', 'group')
Inputs may be any that keep to these rules, and one draw needn't show every extreme that they name: `step_count`: at least 16; some field runs all 32 steps.
All inputs are finite; a program needn't handle non-finite values.
Results may differ from a plain program's by a relative error of at most 0.0039.
The roundings to bfloat16 on the way count: a program that leaves them out, or rounds other values in their place, can miss the bound.
Values may be sent and summed in bfloat16 or wider, within the bound.
A program may use at most 64 MiB of HBM per device.

v0:
```python
import jax
import jax.numpy as jnp
from jax import lax
from jax.sharding import PartitionSpec as P

STEPS = 32


step_rate = 0.125


def padded(x, sides, width):
    for axis, dim in sides:
        count, length = (lax.axis_size(axis), x.shape[dim])
        up = [(i, (i + 1) % count) for i in range(count - 1)]
        down = [(j, i) for i, j in up]
        last = lax.slice_in_dim(x, length - width, length, axis=dim)
        initial = lax.slice_in_dim(x, 0, width, axis=dim)
        before = lax.ppermute(last, axis, up)
        after = lax.ppermute(initial, axis, down)
        x = jnp.concatenate([before, x, after], axis=dim)
    return x


def stencil(current, kappa_rows):
    middle = current[1:-1]
    zero_column = jnp.zeros((middle.shape[0], 1), jnp.float32)
    east_side = jnp.concatenate([middle[:, 1:], zero_column], axis=1)
    west_side = jnp.concatenate([zero_column, middle[:, :-1]], axis=1)
    beside_all = current[2:] + current[:-2] + east_side + west_side
    return middle + step_rate * kappa_rows * (1.0 + 0.25 * jnp.tanh(middle)) * (
        beside_all - 4.0 * middle
    )


def record(history, step_index, inner):
    return lax.dynamic_update_slice_in_dim(history, inner.astype(jnp.bfloat16)[None], step_index, 0)


def contract_rows(left, right):
    return lax.dot_general(
        left, right, (((0,), (0,)), ((), ())), preferred_element_type=jnp.float32
    )


def contract_cols(left, right):
    return lax.dot_general(
        left, right, (((1,), (1,)), ((), ())), preferred_element_type=jnp.float32
    )


def forward(inputs, w_first, w_second, w_third):
    act_a = jnp.tanh(jnp.dot(inputs, w_first, preferred_element_type=jnp.float32))
    hidden_a = act_a.astype(jnp.bfloat16)
    act_b = jnp.tanh(jnp.dot(hidden_a, w_second, preferred_element_type=jnp.float32))
    hidden_b = act_b.astype(jnp.bfloat16)
    act_c = jnp.tanh(jnp.dot(hidden_b, w_third, preferred_element_type=jnp.float32))
    hidden_c = act_c.astype(jnp.bfloat16)
    return ((act_a, act_b, act_c), (hidden_a, hidden_b, hidden_c))


def backward(inputs, activations, hiddens, w_second, w_third, back_c):
    delta_c = (back_c * (1.0 - activations[2] * activations[2])).astype(jnp.bfloat16)
    grad_third = contract_rows(hiddens[1], delta_c)
    back_b = contract_cols(delta_c, w_third)
    delta_b = (back_b * (1.0 - activations[1] * activations[1])).astype(jnp.bfloat16)
    grad_second = contract_rows(hiddens[0], delta_b)
    back_a = contract_cols(delta_b, w_second)
    delta_a = (back_a * (1.0 - activations[0] * activations[0])).astype(jnp.bfloat16)
    grad_first = contract_rows(inputs, delta_a)
    return (grad_first, grad_second, grad_third)


def per_device(
    initial,
    conductivity,
    step_count,
    emit_steps,
    assign,
    sample_inputs,
    w_first,
    w_second,
    w_third,
    w_out,
):
    field_now = initial[0]
    kappa = conductivity[0]
    run_steps = step_count[0]
    emit_row = emit_steps[0]
    row_count = field_now.shape[0]
    start_history = jnp.zeros((STEPS, row_count, field_now.shape[1]), jnp.bfloat16)
    halo_width = 4
    kappa_wide = padded(kappa, (("strip", 0),), halo_width)
    first_row = lax.axis_index("strip") * row_count - halo_width
    global_rows = first_row + jnp.arange(row_count + 2 * halo_width, dtype=jnp.int32)
    inside = ((global_rows >= 0) & (global_rows < row_count * lax.axis_size("strip"))).astype(
        jnp.float32
    )[:, None]

    def block_steps(block_index, carried):
        current, history = carried
        widened = padded(current, (("strip", 0),), halo_width)
        for substep in range(halo_width):
            step_index = block_index * halo_width + substep
            low_row = substep + 1
            span_rows = row_count + 2 * (halo_width - substep - 1)
            candidate = (
                stencil(widened, kappa_wide[low_row : low_row + span_rows])
                * inside[low_row : low_row + span_rows]
            )
            widened = jnp.where(step_index < run_steps, candidate, widened[1:-1])
            offset = halo_width - substep - 1
            history = record(history, step_index, widened[offset : offset + row_count])
        return (widened, history)

    field_now, history = lax.fori_loop(
        0, STEPS // halo_width, block_steps, (field_now, start_history)
    )
    snapshots = jnp.take(history, emit_row - 1, axis=0)
    regrouped = lax.all_to_all(snapshots[None], "group", split_axis=3, concat_axis=0, tiled=True)
    flat_snaps = regrouped.reshape(regrouped.shape[0] * regrouped.shape[1], -1)
    targets = jnp.take(flat_snaps, assign, axis=0)
    weight_flat = w_out.reshape(w_out.shape[0], -1)
    inverse_root = 1.0 / jnp.sqrt(jnp.float32(assign.shape[0]))
    all_inputs = lax.all_gather(sample_inputs, ("group", "strip"), axis=0, tiled=True)
    activations, hiddens = forward(all_inputs, w_first, w_second, w_third)
    hidden_all = hiddens[2]
    predicted = jnp.dot(hidden_all, weight_flat, preferred_element_type=jnp.float32)
    residual = ((predicted - targets.astype(jnp.float32)) * inverse_root).astype(jnp.bfloat16)
    grad_out = contract_rows(hidden_all, residual).astype(jnp.bfloat16)
    residual, grad_out = (residual, grad_out)
    back_c = lax.psum(contract_cols(residual, weight_flat), ("group", "strip"))
    grad_first, grad_second, grad_third = backward(
        all_inputs, activations, hiddens, w_second, w_third, back_c
    )
    return (grad_first, grad_second, grad_third, grad_out.reshape(w_out.shape))


def solution(mesh):
    placed = (
        P("group", "strip", None),
        P("group", "strip", None),
        P("group"),
        P("group", None),
        P(),
        P(("group", "strip"), None),
        P(),
        P(),
        P(),
        P(None, "strip", "group"),
    )
    return jax.shard_map(
        per_device,
        mesh=mesh,
        in_specs=placed,
        out_specs=(P(), P(), P(), P(None, "strip", "group")),
        check_vma=False,
    )
```

profile of v0, /device:TPU:1, one launch (start us, length us, event | category | flops | bytes accessed | tf_op | source)
XLA Modules:
  0.0 374.0 jit_solution(3398122449657235176)
XLA Ops:
  8.9 4.9 %collective-permute-start.2 = (f32[4,1024]{1,0:T(4,128)S(1)}, f32[4,1024]{1,0:T(4,128)S(1)}, u32[]{:S(2)}, u32[]{:S(2)}) collective-permute-start(f32[4,1024]{1,0:T(4,128)S(1)} %get-tuple-element.221), channel_id=1, source_target_pairs={{0,1},{1,2},{2,3},{3,4},{4,5},{5,6},{6,7},{7,8},{8,9},{9,10},{10,1... | collective-permute-start | bytes 49160 | tf_op jit(solution)/shard_map/ppermute | solution.py:19
  20.1 78.7 %while.17 = (s32[]{:T(128)}, f32[32,1024]{1,0:T(8,128)S(1)}, bf16[32,32,1024]{2,1,0:T(8,128)(2,1)S(1)}, s32[]{:T(128)}, f32[40,1024]{1,0:T(8,128)S(1)}, /*index=...) while((s32[]{:T(128)}, f32[32,1024]{1,0:T(8,128)S(1)}, ...), condition=%wide.region_1.2_spmd, body=%wide.region_0.1_spmd.sunk | while | flops 1978390 | bytes 7814625 | solution.py:116
  20.1 2.1 collective-permute-start
  22.2 3.6 collective-permute-start.1
  30.0 2.1 collective-permute-start
  32.0 3.6 collective-permute-start.1
  39.8 2.1 collective-permute-start
  41.9 3.6 collective-permute-start.1
  49.7 2.1 collective-permute-start
  51.7 3.6 collective-permute-start.1
  59.5 2.1 collective-permute-start
  61.6 3.6 collective-permute-start.1
  69.3 2.1 collective-permute-start
  71.4 3.6 collective-permute-start.1
  79.2 2.1 collective-permute-start
  81.2 3.6 collective-permute-start.1
  89.0 2.1 collective-permute-start
  91.1 3.6 collective-permute-start.1
  101.8 4.7 %copy.18 = bf16[1,16,32,1024]{2,1,0,3:T(8,128)(2,1)} copy(bf16[1,16,32,1024]{3,2,1,0:T(8,128)(2,1)S(1)} %bitcast_select_fusion) | data formatting | bytes 2097152 | tf_op jit(solution)/shard_map/jit(_take)/select_n | solution.py:119
  106.5 7.9 %reshape.112 = bf16[8,2,32768]{2,1,0:T(2,128)(2,1)} reshape(bf16[1024,1,16,32]{3,2,1,0:T(8,128)(2,1)} %bitcast.94) | data formatting | bytes 2097152
  114.4 6.7 %all-to-all-start = ((bf16[8,2,32768]{2,1,0:T(2,128)(2,1)}), bf16[8,2,32768]{2,1,0:T(2,128)(2,1)S(1)}, u32[]{:S(2)}, u32[]{:S(2)}) async-start(bf16[8,2,32768]{2,1,0:T(2,128)(2,1)} %reshape.112), calls=%async_computation | async-start | bytes 2097152 | tf_op jit(solution)/shard_map/all_to_all | solution.py:120
  121.1 57.0 %all-gather = bf16[128,4,128]{2,1,0:T(4,128)(2,1)S(1)} all-gather(bf16[1,4,128]{2,1,0:T(4,128)(2,1)S(1)} %bitcast.103), channel_id=1, replica_groups=mesh['group'=8,'strip'=16] {'group','strip'}, dimensions={0}, use_global_device_ids=true | all-gather | bytes 132096 | tf_op jit(solution)/shard_map/all_gather | solution.py:125
  181.3 4.5 %reshape.113 = bf16[1024,1,16,32]{3,2,1,0:T(8,128)(2,1)} reshape(bf16[8,2,32768]{2,1,0:T(2,128)(2,1)S(1)} %all-to-all-done) | data formatting | bytes 2097152
  185.8 5.5 %copy.19 = bf16[1,16,32,8,128]{4,2,1,3,0:T(8,128)(2,1)} copy(bf16[1,16,32,8,128]{2,1,4,3,0:T(8,128)(2,1)} %bitcast.95) | data formatting | bytes 2097152 | tf_op jit(solution)/shard_map/all_to_all | solution.py:120
  193.0 4.4 %gather_fusion.1 = bf16[512,4096]{1,0:T(8,128)(2,1)} fusion(bf16[128,4096]{1,0:T(8,128)(2,1)S(1)} %bitcast.93, s32[1024]{0:T(1024)S(1)} %pad_clamp_fusion), kind=kCustom, calls=%fused_computation.1 | custom fusion | bytes 8390656 | tf_op jit(solution)/shard_map/jit(_take)/gather | solution.py:122
  197.4 6.9 %multiply_convert_fusion = bf16[512,4096]{1,0:T(8,128)(2,1)S(1)} fusion(bf16[512,4096]{1,0:T(8,128)(2,1)} %gather_fusion.1, pred[512]{0:T(512)(128)(4,1)S(1)} %compare_and_fusion.1, bf16[64,8,32,128]{3,2,1,0:T(8,128)(2,1)} %bitcast.104, f32[512,512]{1,0:T(8,128)} %convolution_tanh_fusion), kind=kOutput, calls=%fused_computation.49 | convolution fusion | flops 2158231552 | bytes 13632000 | tf_op jit(solution)/shard_map/dot_general | solution.py:128
  206.3 3.9 %fusion.34 = f32[512,512]{1,0:T(8,128)} fusion(bf16[512,4096]{1,0:T(8,128)(2,1)S(1)} %multiply_convert_fusion, bf16[64,8,32,128]{3,2,1,0:T(8,128)(2,1)S(1)} %bitcast.105), kind=kOutput, calls=%fused_computation.51 | convolution fusion | flops 2147483648 | bytes 9437184 | tf_op jit(solution)/shard_map/dot_general | solution.py:47
  210.2 4.6 %fusion.39 = bf16[64,8,32,128]{3,1,2,0:T(8,128)(2,1)S(1)} fusion(bf16[512,4096]{1,0:T(8,128)(2,1)} %copy-done.5, f32[512,512]{1,0:T(8,128)S(1)} %copy-done.3), kind=kOutput, calls=%fused_computation.56 | convolution fusion | flops 2149842944 | bytes 9437184 | tf_op jit(solution)/shard_map/dot_general | solution.py:41
  214.8 3.3 copy.23
  218.1 139.1 %all-reduce.10.cloned.1.call-done = f32[512,512]{1,0:T(8,128)} async-done(((f32[512,512]{1,0:T(8,128)}), f32[512,512]{1,0:T(8,128)}) %all-reduce.10.cloned.1.call-update) | async-done | bytes 1048592 | tf_op jit(solution)/shard_map/psum | solution.py:132
  360.3 2.1 fusion.43
  362.4 2.5 fusion.52
  (213 shorter events, 34.2 us)
Async XLA Ops:
  7.2 172.8 %copy-start = (bf16[512,512]{1,0:T(8,128)(2,1)S(1)}, bf16[512,512]{1,0:T(8,128)(2,1)}, u32[]{:S(2)}) copy-start(bf16[512,512]{1,0:T(8,128)(2,1)} %param.20) | copy-start | bytes 1572868
  8.9 9.6 %collective-permute-start.2 = (f32[4,1024]{1,0:T(4,128)S(1)}, f32[4,1024]{1,0:T(4,128)S(1)}, u32[]{:S(2)}, u32[]{:S(2)}) collective-permute-start(f32[4,1024]{1,0:T(4,128)S(1)} %get-tuple-element.221), channel_id=1, source_target_pairs={{0,1},{1,2},{2,3},{3,4},{4,5},{5,6},{6,7},{7,8},{8,9},{9,10},{10,1... | collective-permute-start | bytes 49160 | tf_op jit(solution)/shard_map/ppermute | solution.py:19
  13.8 5.1 %collective-permute-start.3 = (f32[4,1024]{1,0:T(4,128)S(1)}, f32[4,1024]{1,0:T(4,128)S(1)}, u32[]{:S(2)}, u32[]{:S(2)}) collective-permute-start(f32[4,1024]{1,0:T(4,128)S(1)} %get-tuple-element.222), channel_id=1, source_target_pairs={{1,0},{2,1},{3,2},{4,3},{5,4},{6,5},{7,6},{8,7},{9,8},{10,9},{11,1... | collective-permute-start | bytes 49160 | tf_op jit(solution)/shard_map/ppermute | solution.py:20
  20.1 9.7 %copy-start.4 = (f32[32,1024]{1,0:T(8,128)S(1)}, f32[32,1024]{1,0:T(8,128)}, u32[]{:S(2)}) copy-start(f32[32,1024]{1,0:T(8,128)} %get-tuple-element.328) | copy-start | bytes 393220 | tf_op jit(solution)/shard_map/while
  20.1 8.6 %collective-permute-start = (f32[4,1024]{1,0:T(4,128)S(1)}, f32[4,1024]{1,0:T(4,128)S(1)}, u32[]{:S(2)}, u32[]{:S(2)}) collective-permute-start(f32[4,1024]{1,0:T(4,128)S(1)} %get-tuple-element.278), channel_id=1, source_target_pairs={{1,0},{2,1},{3,2},{4,3},{5,4},{6,5},{7,6},{8,7},{9,8},{10,9},{11,1... | collective-permute-start | bytes 49160 | tf_op jit(solution)/shard_map/while/body/eval_jaxpr/ppermute | solution.py:20
  22.2 6.6 %collective-permute-start.1 = (f32[4,1024]{1,0:T(4,128)S(1)}, f32[4,1024]{1,0:T(4,128)S(1)}, u32[]{:S(2)}, u32[]{:S(2)}) collective-permute-start(f32[4,1024]{1,0:T(4,128)S(1)} %get-tuple-element.279), channel_id=1, source_target_pairs={{0,1},{1,2},{2,3},{3,4},{4,5},{5,6},{6,7},{7,8},{8,9},{9,10},{10,1... | collective-permute-start | bytes 49160 | tf_op jit(solution)/shard_map/while/body/eval_jaxpr/ppermute | solution.py:19
  29.9 9.7 %copy-start.4 = (f32[32,1024]{1,0:T(8,128)S(1)}, f32[32,1024]{1,0:T(8,128)}, u32[]{:S(2)}) copy-start(f32[32,1024]{1,0:T(8,128)} %get-tuple-element.328) | copy-start | bytes 393220 | tf_op jit(solution)/shard_map/while
  30.0 8.6 %collective-permute-start = (f32[4,1024]{1,0:T(4,128)S(1)}, f32[4,1024]{1,0:T(4,128)S(1)}, u32[]{:S(2)}, u32[]{:S(2)}) collective-permute-start(f32[4,1024]{1,0:T(4,128)S(1)} %get-tuple-element.278), channel_id=1, source_target_pairs={{1,0},{2,1},{3,2},{4,3},{5,4},{6,5},{7,6},{8,7},{9,8},{10,9},{11,1... | collective-permute-start | bytes 49160 | tf_op jit(solution)/shard_map/while/body/eval_jaxpr/ppermute | solution.py:20
  32.0 6.6 %collective-permute-start.1 = (f32[4,1024]{1,0:T(4,128)S(1)}, f32[4,1024]{1,0:T(4,128)S(1)}, u32[]{:S(2)}, u32[]{:S(2)}) collective-permute-start(f32[4,1024]{1,0:T(4,128)S(1)} %get-tuple-element.279), channel_id=1, source_target_pairs={{0,1},{1,2},{2,3},{3,4},{4,5},{5,6},{6,7},{7,8},{8,9},{9,10},{10,1... | collective-permute-start | bytes 49160 | tf_op jit(solution)/shard_map/while/body/eval_jaxpr/ppermute | solution.py:19
  39.8 9.7 %copy-start.4 = (f32[32,1024]{1,0:T(8,128)S(1)}, f32[32,1024]{1,0:T(8,128)}, u32[]{:S(2)}) copy-start(f32[32,1024]{1,0:T(8,128)} %get-tuple-element.328) | copy-start | bytes 393220 | tf_op jit(solution)/shard_map/while
  39.8 8.6 %collective-permute-start = (f32[4,1024]{1,0:T(4,128)S(1)}, f32[4,1024]{1,0:T(4,128)S(1)}, u32[]{:S(2)}, u32[]{:S(2)}) collective-permute-start(f32[4,1024]{1,0:T(4,128)S(1)} %get-tuple-element.278), channel_id=1, source_target_pairs={{1,0},{2,1},{3,2},{4,3},{5,4},{6,5},{7,6},{8,7},{9,8},{10,9},{11,1... | collective-permute-start | bytes 49160 | tf_op jit(solution)/shard_map/while/body/eval_jaxpr/ppermute | solution.py:20
  41.9 6.6 %collective-permute-start.1 = (f32[4,1024]{1,0:T(4,128)S(1)}, f32[4,1024]{1,0:T(4,128)S(1)}, u32[]{:S(2)}, u32[]{:S(2)}) collective-permute-start(f32[4,1024]{1,0:T(4,128)S(1)} %get-tuple-element.279), channel_id=1, source_target_pairs={{0,1},{1,2},{2,3},{3,4},{4,5},{5,6},{6,7},{7,8},{8,9},{9,10},{10,1... | collective-permute-start | bytes 49160 | tf_op jit(solution)/shard_map/while/body/eval_jaxpr/ppermute | solution.py:19
  49.6 9.7 %copy-start.4 = (f32[32,1024]{1,0:T(8,128)S(1)}, f32[32,1024]{1,0:T(8,128)}, u32[]{:S(2)}) copy-start(f32[32,1024]{1,0:T(8,128)} %get-tuple-element.328) | copy-start | bytes 393220 | tf_op jit(solution)/shard_map/while
  49.7 8.6 %collective-permute-start = (f32[4,1024]{1,0:T(4,128)S(1)}, f32[4,1024]{1,0:T(4,128)S(1)}, u32[]{:S(2)}, u32[]{:S(2)}) collective-permute-start(f32[4,1024]{1,0:T(4,128)S(1)} %get-tuple-element.278), channel_id=1, source_target_pairs={{1,0},{2,1},{3,2},{4,3},{5,4},{6,5},{7,6},{8,7},{9,8},{10,9},{11,1... | collective-permute-start | bytes 49160 | tf_op jit(solution)/shard_map/while/body/eval_jaxpr/ppermute | solution.py:20
  51.7 6.6 %collective-permute-start.1 = (f32[4,1024]{1,0:T(4,128)S(1)}, f32[4,1024]{1,0:T(4,128)S(1)}, u32[]{:S(2)}, u32[]{:S(2)}) collective-permute-start(f32[4,1024]{1,0:T(4,128)S(1)} %get-tuple-element.279), channel_id=1, source_target_pairs={{0,1},{1,2},{2,3},{3,4},{4,5},{5,6},{6,7},{7,8},{8,9},{9,10},{10,1... | collective-permute-start | bytes 49160 | tf_op jit(solution)/shard_map/while/body/eval_jaxpr/ppermute | solution.py:19
  59.5 9.7 %copy-start.4 = (f32[32,1024]{1,0:T(8,128)S(1)}, f32[32,1024]{1,0:T(8,128)}, u32[]{:S(2)}) copy-start(f32[32,1024]{1,0:T(8,128)} %get-tuple-element.328) | copy-start | bytes 393220 | tf_op jit(solution)/shard_map/while
  59.5 8.6 %collective-permute-start = (f32[4,1024]{1,0:T(4,128)S(1)}, f32[4,1024]{1,0:T(4,128)S(1)}, u32[]{:S(2)}, u32[]{:S(2)}) collective-permute-start(f32[4,1024]{1,0:T(4,128)S(1)} %get-tuple-element.278), channel_id=1, source_target_pairs={{1,0},{2,1},{3,2},{4,3},{5,4},{6,5},{7,6},{8,7},{9,8},{10,9},{11,1... | collective-permute-start | bytes 49160 | tf_op jit(solution)/shard_map/while/body/eval_jaxpr/ppermute | solution.py:20
  61.6 6.6 %collective-permute-start.1 = (f32[4,1024]{1,0:T(4,128)S(1)}, f32[4,1024]{1,0:T(4,128)S(1)}, u32[]{:S(2)}, u32[]{:S(2)}) collective-permute-start(f32[4,1024]{1,0:T(4,128)S(1)} %get-tuple-element.279), channel_id=1, source_target_pairs={{0,1},{1,2},{2,3},{3,4},{4,5},{5,6},{6,7},{7,8},{8,9},{9,10},{10,1... | collective-permute-start | bytes 49160 | tf_op jit(solution)/shard_map/while/body/eval_jaxpr/ppermute | solution.py:19
  69.3 9.7 %copy-start.4 = (f32[32,1024]{1,0:T(8,128)S(1)}, f32[32,1024]{1,0:T(8,128)}, u32[]{:S(2)}) copy-start(f32[32,1024]{1,0:T(8,128)} %get-tuple-element.328) | copy-start | bytes 393220 | tf_op jit(solution)/shard_map/while
  69.3 8.6 %collective-permute-start = (f32[4,1024]{1,0:T(4,128)S(1)}, f32[4,1024]{1,0:T(4,128)S(1)}, u32[]{:S(2)}, u32[]{:S(2)}) collective-permute-start(f32[4,1024]{1,0:T(4,128)S(1)} %get-tuple-element.278), channel_id=1, source_target_pairs={{1,0},{2,1},{3,2},{4,3},{5,4},{6,5},{7,6},{8,7},{9,8},{10,9},{11,1... | collective-permute-start | bytes 49160 | tf_op jit(solution)/shard_map/while/body/eval_jaxpr/ppermute | solution.py:20
  71.4 6.6 %collective-permute-start.1 = (f32[4,1024]{1,0:T(4,128)S(1)}, f32[4,1024]{1,0:T(4,128)S(1)}, u32[]{:S(2)}, u32[]{:S(2)}) collective-permute-start(f32[4,1024]{1,0:T(4,128)S(1)} %get-tuple-element.279), channel_id=1, source_target_pairs={{0,1},{1,2},{2,3},{3,4},{4,5},{5,6},{6,7},{7,8},{8,9},{9,10},{10,1... | collective-permute-start | bytes 49160 | tf_op jit(solution)/shard_map/while/body/eval_jaxpr/ppermute | solution.py:19
  79.2 9.7 %copy-start.4 = (f32[32,1024]{1,0:T(8,128)S(1)}, f32[32,1024]{1,0:T(8,128)}, u32[]{:S(2)}) copy-start(f32[32,1024]{1,0:T(8,128)} %get-tuple-element.328) | copy-start | bytes 393220 | tf_op jit(solution)/shard_map/while
  79.2 8.6 %collective-permute-start = (f32[4,1024]{1,0:T(4,128)S(1)}, f32[4,1024]{1,0:T(4,128)S(1)}, u32[]{:S(2)}, u32[]{:S(2)}) collective-permute-start(f32[4,1024]{1,0:T(4,128)S(1)} %get-tuple-element.278), channel_id=1, source_target_pairs={{1,0},{2,1},{3,2},{4,3},{5,4},{6,5},{7,6},{8,7},{9,8},{10,9},{11,1... | collective-permute-start | bytes 49160 | tf_op jit(solution)/shard_map/while/body/eval_jaxpr/ppermute | solution.py:20
  81.2 6.6 %collective-permute-start.1 = (f32[4,1024]{1,0:T(4,128)S(1)}, f32[4,1024]{1,0:T(4,128)S(1)}, u32[]{:S(2)}, u32[]{:S(2)}) collective-permute-start(f32[4,1024]{1,0:T(4,128)S(1)} %get-tuple-element.279), channel_id=1, source_target_pairs={{0,1},{1,2},{2,3},{3,4},{4,5},{5,6},{6,7},{7,8},{8,9},{9,10},{10,1... | collective-permute-start | bytes 49160 | tf_op jit(solution)/shard_map/while/body/eval_jaxpr/ppermute | solution.py:19
  89.0 8.6 %collective-permute-start = (f32[4,1024]{1,0:T(4,128)S(1)}, f32[4,1024]{1,0:T(4,128)S(1)}, u32[]{:S(2)}, u32[]{:S(2)}) collective-permute-start(f32[4,1024]{1,0:T(4,128)S(1)} %get-tuple-element.278), channel_id=1, source_target_pairs={{1,0},{2,1},{3,2},{4,3},{5,4},{6,5},{7,6},{8,7},{9,8},{10,9},{11,1... | collective-permute-start | bytes 49160 | tf_op jit(solution)/shard_map/while/body/eval_jaxpr/ppermute | solution.py:20
  91.1 6.6 %collective-permute-start.1 = (f32[4,1024]{1,0:T(4,128)S(1)}, f32[4,1024]{1,0:T(4,128)S(1)}, u32[]{:S(2)}, u32[]{:S(2)}) collective-permute-start(f32[4,1024]{1,0:T(4,128)S(1)} %get-tuple-element.279), channel_id=1, source_target_pairs={{0,1},{1,2},{2,3},{3,4},{4,5},{5,6},{6,7},{7,8},{8,9},{9,10},{10,1... | collective-permute-start | bytes 49160 | tf_op jit(solution)/shard_map/while/body/eval_jaxpr/ppermute | solution.py:19
  106.5 14.6 %copy-start.8 = (bf16[4,128]{1,0:T(4,128)(2,1)S(1)}, bf16[4,128]{1,0:T(4,128)(2,1)}, u32[]{:S(2)}) copy-start(bf16[4,128]{1,0:T(4,128)(2,1)} %param.17) | copy-start | bytes 3076
  106.5 71.7 %copy-start.7 = (bf16[128,512]{1,0:T(8,128)(2,1)S(1)}, bf16[128,512]{1,0:T(8,128)(2,1)}, u32[]{:S(2)}) copy-start(bf16[128,512]{1,0:T(8,128)(2,1)} %param.18) | copy-start | bytes 393220
  106.5 71.9 %copy-start.6 = (bf16[512,512]{1,0:T(8,128)(2,1)S(1)}, bf16[512,512]{1,0:T(8,128)(2,1)}, u32[]{:S(2)}) copy-start(bf16[512,512]{1,0:T(8,128)(2,1)} %param.19) | copy-start | bytes 1572868
  114.4 66.9 %all-to-all-start = ((bf16[8,2,32768]{2,1,0:T(2,128)(2,1)}), bf16[8,2,32768]{2,1,0:T(2,128)(2,1)S(1)}, u32[]{:S(2)}, u32[]{:S(2)}) async-start(bf16[8,2,32768]{2,1,0:T(2,128)(2,1)} %reshape.112), calls=%async_computation | async-start | bytes 2097152 | tf_op jit(solution)/shard_map/all_to_all | solution.py:120
  121.1 236.1 %all-reduce.10.cloned.1.call-start = ((), (), s32[]{:S(2)}) async-start(), calls=%async_computation.1 | async-start | bytes 2097152 | tf_op jit(solution)/shard_map/psum | solution.py:132
  214.8 144.2 %copy-start.2 = (f32[512,512]{1,0:T(8,128)S(1)}, f32[512,512]{1,0:T(8,128)}, u32[]{:S(2)}) copy-start(f32[512,512]{1,0:T(8,128)} %copy-done.1) | copy-start | bytes 3145732
  (5 other events, 25.5 us)
Sparse Core Ops, SparseCore 0:
  210.3 146.8 all-reduce.9
where the time goes:
time: 376 us; the launch traced here: 374 us
  waiting for transfers between devices  140 us (37%)
  starting transfers between devices  59.1 us (16%)
  blocking collectives  57 us (15%)
  local copies, waits for them, and re-layouts  45.6 us (12%)
  matrix products  24.8 us (7%)
  loops' own time  22.1 us (6%)
  between operations  14.2 us (4%)
  other arithmetic  11.6 us (3%)
    psum x1, waiting for transfers between devices, per_device(): back_c = lax.psum(contract_cols(residual, weight_flat), ('group', 'strip'))  139 us
    all_gather x1, blocking collectives, per_device(): lax.all_gather(sample_inputs, ('group', 'strip'), axis=0, tiled=True)  57 us
    ppermute x9, starting transfers between devices, padded(): before = lax.ppermute(last, axis, up)  34 us
    another operation x1, loops' own time, per_device(): lax.fori_loop(0, STEPS // halo_width, block_steps, (field_now, start_hist...  22.1 us
    unnamed x24, local copies, waits for them, and re-layouts  22.1 us
    ppermute x9, starting transfers between devices, padded(): after = lax.ppermute(initial, axis, down)  18.3 us
    dot_general x4, matrix products, contract_rows(): lax.dot_general(left, right, (((0,), (0,)), ((), ())), preferred_element_...  10.6 us
  transfers between devices with their start and end apart: 20, of which 2 were waited for; matrix products, arithmetic and copies ran while one was open for 4% of the time, Pallas kernels for 0%

commit v1 on v0

v1 whole, which is shorter than its diff:
```python
import jax
import jax.numpy as jnp
from jax import lax
from jax.experimental import pallas as pl
from jax.experimental.pallas import tpu as pltpu
from jax.sharding import PartitionSpec as P

MESH = pl.DeviceIdType.MESH
F32, BF16 = jnp.float32, jnp.bfloat16
STEPS, SNAPS, ROWS, HID, FEAT = 32, 16, 32, 512, 128
GROUPS, STRIPS = 8, 16
DEVS, CHIPS = GROUPS * STRIPS, GROUPS * STRIPS // 2
REGION = 3 * ROWS
PAIRS = ROWS // 2
CHUNK = 4


def dot(a, b):
    return jnp.dot(a, b, preferred_element_type=F32)


def dot_nt(a, b):
    return lax.dot_general(a, b, (((1,), (1,)), ((), ())), preferred_element_type=F32)


def swap_matrix():
    row = lax.broadcasted_iota(jnp.int32, (256, 256), 0)
    col = lax.broadcasted_iota(jnp.int32, (256, 256), 1)
    return jnp.where((row % 16) * 16 + row // 16 == col, 1.0, 0.0).astype(BF16)


def main_kernel(
    initial, conductivity, step_count, emit_steps, assign, sample_inputs,
    w_first, w_second, w_third, w_out,
    gout_hbm, acta_hbm, actb_hbm, hat_hbm, hbt_hbm, xt_hbm, delta_hbm,
    land_u, land_k, state_a, state_b, kap, hist, tmp, send, snaps, part, gath,
    raw, w2, pred, resid, acc, pair_in, pieces, delta, act_a, act_b, act_c, hat, hbt, hct, xt, hidc, onehot,
    wf, ws, wt,
    halo_send, halo_recv, part_send, part_recv, gath_send, gath_recv, snap_send, snap_recv,
    pair_send, pair_recv, piece_send, piece_recv, delta_send, delta_recv, twin_send, twin_recv,
    w_sem, raw_sem, own_sem, out_sem,
):
    g, s = lax.axis_index("group"), lax.axis_index("strip")
    me = g * STRIPS + s
    core = s % 2
    chip = g * (STRIPS // 2) + s // 2
    twin = (g, s + 1 - 2 * core)

    def remote(src, dst, send_sem, recv_sem, device):
        return pltpu.make_async_remote_copy(
            src_ref=src, dst_ref=dst, send_sem=send_sem, recv_sem=recv_sem, device_id=device, device_id_type=MESH
        )

    barrier = pltpu.get_barrier_semaphore()

    @pl.loop(1, DEVS)
    def _(i):
        peer = (me + i) % DEVS
        pl.semaphore_signal(barrier, inc=1, device_id=(peer // STRIPS, peer % STRIPS), device_id_type=MESH)

    raw_copies = [
        pltpu.make_async_copy(w_out.at[pl.ds(64 * i, 64)], raw.at[pl.ds(64 * i, 64)], raw_sem.at[i]) for i in range(8)
    ]
    for copy in raw_copies:
        copy.start()
    weight_copies = [
        pltpu.make_async_copy(a, b, w_sem.at[i]) for i, (a, b) in enumerate(((w_first, wf), (w_second, ws), (w_third, wt)))
    ]
    for copy in weight_copies:
        copy.start()

    def spread(ref, first_row, x):
        for j in range(8):
            ref[pl.ds(first_row * 8 + j, ROWS, stride=8), :] = x[:, j * 128 : (j + 1) * 128]

    spread(state_a, ROWS, initial[0])
    spread(kap, ROWS, 0.125 * conductivity[0])
    quad = s % 4
    part[quad, 0:4, :] = sample_inputs[...].astype(F32)
    ids = lax.broadcasted_iota(jnp.int32, (DEVS, HID), 0)
    onehot[...] = jnp.transpose(jnp.where(ids == assign[...], 1.0, 0.0)).astype(BF16)
    swap = swap_matrix()

    pl.semaphore_wait(barrier, DEVS - 1)

    above, below = (g, jnp.maximum(s - 1, 0)), (g, jnp.minimum(s + 1, STRIPS - 1))
    up_copies = [
        remote(initial.at[0], land_u.at[1], halo_send.at[0], halo_recv.at[0], above),
        remote(conductivity.at[0], land_k.at[1], halo_send.at[1], halo_recv.at[1], above),
    ]
    down_copies = [
        remote(initial.at[0], land_u.at[0], halo_send.at[2], halo_recv.at[2], below),
        remote(conductivity.at[0], land_k.at[0], halo_send.at[3], halo_recv.at[3], below),
    ]

    @pl.when(s > 0)
    def _():
        for copy in up_copies:
            copy.start()

    @pl.when(s < STRIPS - 1)
    def _():
        for copy in down_copies:
            copy.start()

    for i in range(1, 4):
        remote(part.at[quad], part.at[quad], part_send, part_recv, (g, s - quad + (quad + i) % 4)).start()

    def relayout_weights(i, carry):
        for half in range(2):
            k0 = pl.multiple_of((i * 2 + half) * 16, 16)
            x = jnp.concatenate([raw[pl.ds(k0, 16), b * 16 : b * 16 + 16, :].reshape(256, 128) for b in range(2)], axis=1)
            y = dot(swap, x).astype(BF16)
            for b in range(2):
                for r in range(16):
                    row = b * 16 + r
                    w2[row // 2, pl.ds(k0, 16), (row % 2) * 128 : (row % 2) * 128 + 128] = y[
                        r * 16 : r * 16 + 16, b * 128 : b * 128 + 128
                    ]
        return carry

    for i, copy in enumerate(raw_copies):
        copy.wait()
    lax.fori_loop(0, 16, relayout_weights, 0)

    remote(part.at[pl.ds(0, 3)], part.at[pl.ds(0, 3)], part_send, part_recv, twin).wait()
    low = lax.broadcasted_iota(jnp.int32, (8, 128), 0) < 4
    tile = jnp.concatenate(
        [jnp.where(low, part[2 * i], pltpu.roll(part[2 * i + 1], 4, axis=0)) for i in range(2)], axis=0
    )
    mine = g * 4 + s // 4
    gath[mine] = tile.astype(BF16)

    @pl.loop(1, 32)
    def _(i):
        other = (mine + i) % 32
        remote(gath.at[mine], gath.at[mine], gath_send, gath_recv, (other // 4, (other % 4) * 4 + quad)).start()

    def land(has, copies_in, first_row, side):
        @pl.when(has)
        def _():
            for copy in copies_in:
                copy.wait_recv()
            spread(state_a, first_row, land_u[side])
            spread(kap, first_row, 0.125 * land_k[side])

        @pl.when(jnp.logical_not(has))
        def _():
            zero = jnp.zeros((ROWS * 8, 128), F32)
            state_a[pl.ds(first_row * 8, ROWS * 8), :] = zero
            kap[pl.ds(first_row * 8, ROWS * 8), :] = zero

    land(s > 0, down_copies, 0, 0)
    land(s < STRIPS - 1, up_copies, 2 * ROWS, 1)

    lane = lax.broadcasted_iota(jnp.int32, (8, 128), 1)
    sub = lax.broadcasted_iota(jnp.int32, (8, 128), 0)
    first_lane, last_lane = lane == 0, lane == 127
    west_end, east_end = first_lane & (sub == 0), last_lane & (sub == 7)

    def step(src, dst, first, last, t):
        prev = src[(first - 1) * 8 : first * 8, :]
        here = src[first * 8 : first * 8 + 8, :]
        for r in range(first, last + 1):
            after = src[(r + 1) * 8 : (r + 2) * 8, :]
            w = pltpu.roll(here, 1, axis=1)
            w = jnp.where(west_end, 0.0, jnp.where(first_lane, pltpu.roll(w, 1, axis=0), w))
            e = pltpu.roll(here, 127, axis=1)
            e = jnp.where(east_end, 0.0, jnp.where(last_lane, pltpu.roll(e, 7, axis=0), e))
            beside = (after + prev) + (e + w)
            new = here + kap[r * 8 : r * 8 + 8, :] * (1.0 + 0.25 * jnp.tanh(here)) * (beside - 4.0 * here)
            dst[r * 8 : r * 8 + 8, :] = new
            if ROWS <= r < 2 * ROWS:
                hist[t * ROWS + (r - ROWS)] = new
            prev, here = here, after

    for phase in range(8):
        first, last = 4 * phase + 1, REGION - 2 - 4 * phase

        @pl.loop(2 * phase, 2 * phase + 2)
        def _(i):
            step(state_a, state_b, first, last, 2 * i)
            step(state_b, state_a, first, last, 2 * i + 1)

    count = step_count[0]
    bases = [jnp.maximum(jnp.minimum(emit_steps[0, k], count) - 1, 0) * ROWS for k in range(SNAPS)]

    def pack(rp, carry):
        for h in range(2):
            for k in range(SNAPS):
                tmp[h, pl.ds(k, 8, stride=16), :] = hist[bases[k] + (2 * rp + h)]
            for to in range(GROUPS):
                send[to, rp, :, h * 128 : h * 128 + 128] = tmp[h, to * 16 : to * 16 + 16, :].astype(BF16)
        return carry

    def snap_copy(c, to):
        rows = pl.ds(c * CHUNK, CHUNK)
        return remote(
            send.at[to, rows],
            snaps.at[rows, pl.ds(pl.multiple_of(g * SNAPS, SNAPS), SNAPS), :],
            snap_send,
            snap_recv.at[c],
            (to, s),
        )

    for c in range(PAIRS // CHUNK):
        lax.fori_loop(c * CHUNK, (c + 1) * CHUNK, pack, 0)

        @pl.loop(1, GROUPS)
        def _(i):
            snap_copy(c, (g + i) % GROUPS).start()

    own = pltpu.make_async_copy(
        send.at[g], snaps.at[:, pl.ds(pl.multiple_of(g * SNAPS, SNAPS), SNAPS), :], own_sem
    )
    own.start()

    for copy in weight_copies:
        copy.wait()
    remote(gath.at[pl.ds(0, 31)], gath.at[pl.ds(0, 31)], gath_send, gath_recv, twin).wait()

    @pl.loop(0, 4)
    def _(m):
        rows = pl.ds(pl.multiple_of(m * 128, 128), 128)
        x = gath[pl.ds(m * 8, 8)].reshape(128, FEAT)
        xt[:, rows] = jnp.transpose(x.astype(F32)).astype(BF16)
        a = jnp.tanh(dot(x, wf[...]))
        act_a[rows, :] = a
        hat[:, rows] = jnp.transpose(a).astype(BF16)
        b = jnp.tanh(dot(a.astype(BF16), ws[...]))
        act_b[rows, :] = b
        hbt[:, rows] = jnp.transpose(b).astype(BF16)
        c = jnp.tanh(dot(b.astype(BF16), wt[...]))
        hct[:, rows] = jnp.transpose(c).astype(BF16)
        hidc[rows, :] = c.astype(BF16)
        for kb in range(4):
            act_c[pl.ds(kb * 32 + m * 8, 8)] = c[:, kb * 128 : kb * 128 + 128].reshape(8, 16, 128)

    outs = [
        pltpu.make_async_copy(a, b, out_sem.at[i])
        for i, (a, b) in enumerate(((act_a, acta_hbm), (act_b, actb_hbm), (hat, hat_hbm), (hbt, hbt_hbm), (xt, xt_hbm)))
    ]
    for copy in outs:
        copy.start()

    @pl.loop(0, PAIRS)
    def _(rp):
        pred[rp] = dot(hidc[...], w2[rp])

    own.wait()
    inverse_root = F32(1.0) / jnp.sqrt(F32(HID))

    def residual_chunk(c):
        remote(snaps.at[pl.ds(0, CHUNK), pl.ds(0, 112), :], snaps.at[pl.ds(0, CHUNK), pl.ds(0, 112), :],
               snap_send, snap_recv.at[c], twin).wait_recv()

        @pl.loop(c * CHUNK, (c + 1) * CHUNK)
        def _(rp):
            resid[rp] = ((pred[rp] - dot(onehot[...], snaps[rp])) * inverse_root).astype(BF16)

    def back_half(c, half, fresh):
        left = jnp.concatenate([resid[c * CHUNK + i] for i in range(CHUNK)], axis=1)
        k0 = pl.multiple_of(half * 256, 256)
        right = jnp.concatenate([w2[c * CHUNK + i, pl.ds(k0, 256), :] for i in range(CHUNK)], axis=1)
        value = dot_nt(left, right)
        for kb in range(2):
            at = pl.ds(half * 64 + kb * 32, 32)
            v = value[:, kb * 128 : kb * 128 + 128].reshape(32, 16, 128)
            acc[at] = v if fresh else acc[at] + v

    residual_chunk(0)
    back_half(0, 1 - core, True)
    back_half(0, core, True)

    @pl.loop(1, 3)
    def _(c):
        residual_chunk(c)
        back_half(c, 1 - core, False)
        back_half(c, core, False)

    residual_chunk(3)
    back_half(3, 1 - core, False)
    theirs = pl.ds((1 - core) * 64, 64)
    to_twin = remote(acc.at[theirs], pair_in, pair_send, pair_recv, twin)
    to_twin.start()
    back_half(3, core, False)
    to_twin.wait_recv()

    @pl.loop(0, 8)
    def _(i):
        at = pl.ds(core * 64 + i * 8, 8)
        acc[at] = acc[at] + pair_in[pl.ds(i * 8, 8)]

    @pl.loop(1, CHIPS)
    def _(i):
        p = (chip + i) % CHIPS
        remote(acc.at[core * 64 + p], pieces.at[chip], piece_send, piece_recv, (p // 8, (p % 8) * 2 + core)).start()

    pieces[chip] = acc[core * 64 + chip]

    @pl.loop(0, PAIRS)
    def _(rp):
        w2[rp] = dot(hct[...], resid[rp]).astype(BF16)

    remote(pieces.at[pl.ds(0, 63)], pieces.at[pl.ds(0, 63)], piece_send, piece_recv, twin).wait_recv()
    total = pieces[0]
    for i in range(1, CHIPS):
        total = total + pieces[i]
    a = act_c[core * 64 + chip]
    delta[core * 64 + chip] = (total * (1.0 - a * a)).astype(BF16)

    @pl.loop(1, CHIPS)
    def _(i):
        p = (chip + i) % CHIPS
        at = core * 64 + chip
        remote(delta.at[at], delta.at[at], delta_send, delta_recv, (p // 8, (p % 8) * 2 + core)).start()

    def relayout_grad(i, carry):
        for half in range(2):
            k0 = pl.multiple_of((i * 2 + half) * 16, 16)
            x = jnp.concatenate(
                [
                    jnp.concatenate(
                        [w2[b * 8 + r // 2, pl.ds(k0, 16), (r % 2) * 128 : (r % 2) * 128 + 128] for r in range(16)], axis=0
                    )
                    for b in range(2)
                ],
                axis=1,
            )
            y = dot(swap, x).astype(BF16)
            for b in range(2):
                raw[pl.ds(k0, 16), b * 16 : b * 16 + 16, :] = y[:, b * 128 : b * 128 + 128].reshape(16, 16, 128)
        return carry

    lax.fori_loop(0, 16, relayout_grad, 0)
    grad_copy = pltpu.make_async_copy(raw, gout_hbm, out_sem.at[5])
    grad_copy.start()

    remote(delta.at[pl.ds(0, 63)], delta.at[pl.ds(0, 63)], delta_send, delta_recv, twin).wait_recv()
    ours = pl.ds(core * 64, 64)
    to_twin2 = remote(delta.at[ours], delta.at[ours], twin_send, twin_recv, twin)
    to_twin2.start()
    to_twin2.wait_recv()
    delta_copy = pltpu.make_async_copy(delta, delta_hbm, out_sem.at[6])
    delta_copy.start()

    @pl.when(s > 0)
    def _():
        for copy in up_copies:
            copy.wait_send()

    @pl.when(s < STRIPS - 1)
    def _():
        for copy in down_copies:
            copy.wait_send()

    remote(send.at[pl.ds(0, 7)], send.at[pl.ds(0, 7)], snap_send, snap_recv.at[0], twin).wait_send()
    to_twin.wait_send()
    remote(pieces.at[pl.ds(0, 63)], pieces.at[pl.ds(0, 63)], piece_send, piece_recv, twin).wait_send()
    remote(delta.at[pl.ds(0, 63)], delta.at[pl.ds(0, 63)], delta_send, delta_recv, twin).wait_send()
    to_twin2.wait_send()
    for copy in outs:
        copy.wait()
    grad_copy.wait()
    delta_copy.wait()


def final_kernel(
    gout_in, acta_in, actb_in, hat_in, hbt_in, xt_in, delta_in, ws_in, wt_in,
    g1_out, g2_out, g3_out, gout_out,
    stage, act_a, act_b, hat, hbt, xt, delta, ws, wt, g1, g2, g3, in_sem, stage_in, stage_out, out_sem,
):
    loads = [
        pltpu.make_async_copy(a, b, in_sem.at[i])
        for i, (a, b) in enumerate((
            (delta_in, delta), (hbt_in, hbt), (wt_in, wt), (actb_in, act_b), (hat_in, hat), (ws_in, ws),
            (acta_in, act_a), (xt_in, xt),
        ))
    ]
    for copy in loads:
        copy.start()
    parts = [pl.ds(i * 64, 64) for i in range(8)]
    ins = [pltpu.make_async_copy(gout_in.at[p], stage.at[p], stage_in.at[i]) for i, p in enumerate(parts)]
    outs = [pltpu.make_async_copy(stage.at[p], gout_out.at[p], stage_out.at[i]) for i, p in enumerate(parts)]
    for copy in ins:
        copy.start()
    for copy in loads[:3]:
        copy.wait()
    dc = jnp.concatenate([delta[i * 32 : i * 32 + 32].reshape(HID, 128) for i in range(4)], axis=1)
    g3[...] = dot(hbt[...], dc)
    to_g3 = pltpu.make_async_copy(g3, g3_out, out_sem.at[0])
    to_g3.start()
    for a, b in zip(ins, outs):
        a.wait()
        b.start()
    loads[3].wait()
    db = (dot_nt(dc, wt[...]) * (1.0 - act_b[...] * act_b[...])).astype(BF16)
    loads[4].wait()
    g2[...] = dot(hat[...], db)
    to_g2 = pltpu.make_async_copy(g2, g2_out, out_sem.at[1])
    to_g2.start()
    loads[5].wait()
    loads[6].wait()
    da = (dot_nt(db, ws[...]) * (1.0 - act_a[...] * act_a[...])).astype(BF16)
    loads[7].wait()
    g1[...] = dot(xt[...], da)
    to_g1 = pltpu.make_async_copy(g1, g1_out, out_sem.at[2])
    to_g1.start()
    for copy in outs + [to_g3, to_g2, to_g1]:
        copy.wait()


def per_device(initial, conductivity, step_count, emit_steps, assign, sample_inputs, w_first, w_second, w_third, w_out):
    vmem, smem = pl.BlockSpec(memory_space=pltpu.VMEM), pl.BlockSpec(memory_space=pltpu.SMEM)
    hbm = pl.BlockSpec(memory_space=pl.ANY)
    shape = jax.ShapeDtypeStruct
    dma = pltpu.SemaphoreType.DMA
    mats = (
        shape((HID, HID), F32), shape((HID, HID), F32), shape((HID, HID), BF16), shape((HID, HID), BF16),
        shape((FEAT, HID), BF16), shape((DEVS, 16, 128), BF16),
    )
    gout, *kept = pl.pallas_call(
        main_kernel,
        out_shape=(shape((HID, ROWS, 128), BF16),) + mats,
        in_specs=[vmem, vmem, smem, smem, vmem, vmem, hbm, hbm, hbm, hbm],
        out_specs=[hbm] * 7,
        scratch_shapes=[
            pltpu.VMEM((2, ROWS, 1024), F32), pltpu.VMEM((2, ROWS, 1024), F32),
            pltpu.VMEM((REGION * 8, 128), F32), pltpu.VMEM((REGION * 8, 128), F32), pltpu.VMEM((REGION * 8, 128), F32),
            pltpu.VMEM((STEPS * ROWS, 8, 128), F32),
            pltpu.VMEM((2, 128, 128), F32),
            pltpu.VMEM((GROUPS, PAIRS, SNAPS, 256), BF16),
            pltpu.VMEM((PAIRS, DEVS, 256), BF16),
            pltpu.VMEM((4, 8, 128), F32),
            pltpu.VMEM((32, 16, 128), BF16),
            pltpu.VMEM((HID, ROWS, 128), BF16),
            pltpu.VMEM((PAIRS, HID, 256), BF16),
            pltpu.VMEM((PAIRS, HID, 256), F32),
            pltpu.VMEM((PAIRS, HID, 256), BF16),
            pltpu.VMEM((DEVS, 16, 128), F32),
            pltpu.VMEM((64, 16, 128), F32),
            pltpu.VMEM((CHIPS, 16, 128), F32),
            pltpu.VMEM((DEVS, 16, 128), BF16),
            pltpu.VMEM((HID, HID), F32), pltpu.VMEM((HID, HID), F32), pltpu.VMEM((DEVS, 16, 128), F32),
            pltpu.VMEM((HID, HID), BF16), pltpu.VMEM((HID, HID), BF16), pltpu.VMEM((HID, HID), BF16),
            pltpu.VMEM((FEAT, HID), BF16), pltpu.VMEM((HID, HID), BF16), pltpu.VMEM((HID, DEVS), BF16),
            pltpu.VMEM((FEAT, HID), BF16), pltpu.VMEM((HID, HID), BF16), pltpu.VMEM((HID, HID), BF16),
            dma((4,)), dma((4,)), dma, dma, dma, dma, dma, dma((4,)),
            dma, dma, dma, dma, dma, dma, dma, dma,
            dma((3,)), dma((8,)), dma, dma((7,)),
        ],
        compiler_params=pltpu.CompilerParams(
            collective_id=0, has_side_effects=True, vmem_limit_bytes=60 * 1024 * 1024
        ),
        name="solve_and_reduce",
    )(
        initial, conductivity, step_count, emit_steps, assign.reshape(1, HID), sample_inputs,
        w_first, w_second, w_third, w_out,
    )
    outs = pl.pallas_call(
        final_kernel,
        out_shape=(shape((FEAT, HID), F32), shape((HID, HID), F32), shape((HID, HID), F32), shape((HID, ROWS, 128), BF16)),
        in_specs=[hbm] * 9,
        out_specs=[hbm] * 4,
        scratch_shapes=[
            pltpu.VMEM((HID, ROWS, 128), BF16), pltpu.VMEM((HID, HID), F32), pltpu.VMEM((HID, HID), F32),
            pltpu.VMEM((HID, HID), BF16), pltpu.VMEM((HID, HID), BF16), pltpu.VMEM((FEAT, HID), BF16),
            pltpu.VMEM((DEVS, 16, 128), BF16), pltpu.VMEM((HID, HID), BF16), pltpu.VMEM((HID, HID), BF16),
            pltpu.VMEM((FEAT, HID), F32), pltpu.VMEM((HID, HID), F32), pltpu.VMEM((HID, HID), F32),
            dma((8,)), dma((8,)), dma((8,)), dma((3,)),
        ],
        name="outputs",
        compiler_params=pltpu.CompilerParams(vmem_limit_bytes=63 * 1024 * 1024),
    )(gout, *kept, w_second, w_third)
    return tuple(outs)


def solution(mesh):
    placed = (
        P("group", "strip", None), P("group", "strip", None), P("group"), P("group", None), P(),
        P(("group", "strip"), None), P(), P(), P(), P(None, "strip", "group"),
    )
    return jax.shard_map(
        per_device, mesh=mesh, in_specs=placed, out_specs=(P(), P(), P(), P(None, "strip", "group")), check_vma=False
    )
```

time: 376 us -> 71 us (0.19)
  waiting for transfers between devices: 140 us -> 0 us
  Pallas kernels: 0 us -> 69.6 us
  starting transfers between devices: 59.1 us -> 0 us
  blocking collectives: 57 us -> 0 us
  local copies, waits for them, and re-layouts: 45.6 us -> 0 us
  matrix products: 24.8 us -> 0 us
  loops' own time: 22.1 us -> 0 us
  between operations: 14.2 us -> 1.29 us
  other arithmetic: 11.6 us -> 0 us
    psum x1 -> x0, waiting for transfers between devices: 139 us -> none  [per_device(): back_c = lax.psum(contract_cols(residual, weight_flat), ('group', 'strip'))]
    pallas_call x0 -> x2, Pallas kernels: none -> 69.6 us  [the longest x1 62.1 us: per_device(): pl.pallas_call(main_kernel, out_shape=(shape((HID, ROWS, 128), BF16),) +...]
    all_gather x1 -> x0, blocking collectives: 57 us -> none  [per_device(): lax.all_gather(sample_inputs, ('group', 'strip'), axis=0, tiled=True)]
    ppermute x18 -> x0, starting transfers between devices: 52.4 us -> none  [the longest x9 34 us: padded(): before = lax.ppermute(last, axis, up)]
    dot_general x10 -> x0, matrix products: 24.8 us -> none  [the longest x4 10.6 us: contract_rows(): lax.dot_general(left, right, (((0,), (0,)), ((), ())), preferred_element_...]
    another operation x1 -> x0, loops' own time: 22.1 us -> none  [per_device(): lax.fori_loop(0, STEPS // halo_width, block_steps, (field_now, start_hist...]
    unnamed x24 -> x0, local copies, waits for them, and re-layouts: 22.1 us -> none
    all_to_all x1 -> x0, starting transfers between devices: 6.65 us -> none  [per_device(): lax.all_to_all(snapshots[None], 'group', split_axis=3, concat_axis=0, til...]
  transfers between devices with their start and end apart: 20 -> 0, of which waited for: 2 -> 0; matrix products, arithmetic and copies ran while one was open for 4% -> 0% of each run, Pallas kernels for 0% -> 0%
where the time goes in v1:
time: 71 us; the launch traced here: 70.9 us
  Pallas kernels  69.6 us (98%)
  between operations  1.29 us (2%)
    pallas_call x1, Pallas kernels, per_device(): pl.pallas_call(main_kernel, out_shape=(shape((HID, ROWS, 128), BF16),) +...  62.1 us
    pallas_call x1, Pallas kernels, per_device(): pl.pallas_call(final_kernel, out_shape=(shape((FEAT, HID), F32), shape((H...  7.47 us

profile of v1, /device:TPU:1, one launch (start us, length us, event | category | flops | bytes accessed | tf_op | source)
XLA Modules:
  0.0 70.9 jit_solution(4466370093707230021)
XLA Ops:
  1.3 62.1 %solve_and_reduce.1 = (bf16[512,32,128]{2,1,0:T(8,128)(2,1)}, f32[512,512]{1,0:T(8,128)}, f32[512,512]{1,0:T(8,128)}, bf16[512,512]{1,0:T(8,128)(2,1)}, bf16[512...) custom-call(f32[1,32,1024]{2,1,0:T(8,128)} %initial.1, f32[1,32,1024]{2,1,0:T(8,128)} %conductivity.1, ...), custom_call_target="tpu_custom_call" | custom-call | tf_op jit(solution)/shard_map/solve_and_reduce/pallas_call | solution.py:422
  63.4 7.5 %outputs.1 = (f32[128,512]{1,0:T(8,128)}, f32[512,512]{1,0:T(8,128)}, f32[512,512]{1,0:T(8,128)}, bf16[512,32,128]{2,1,0:T(8,128)(2,1)}) custom-call(bf16[512,32,128]{2,1,0:T(8,128)(2,1)} %get-tuple-element.11.gout_in, f32[512,512]{1,0:T(8,128)} %get-tuple-element.12.acta_in, f32[512,512]{1,0:T(8,128)} %get-tuple-element.13.actb_in, ...), custom_call_target="tpu_custom_call" | custom-call | tf_op jit(solution)/shard_map/outputs/pallas_call | solution.py:460

commit v2 on v1

v2 whole, which is shorter than its diff:
```python
import jax
import jax.numpy as jnp
from jax import lax
from jax.experimental import pallas as pl
from jax.experimental.pallas import tpu as pltpu
from jax.sharding import PartitionSpec as P

FLAT = pl.DeviceIdType.LOGICAL
F32, BF16 = jnp.float32, jnp.bfloat16
STEPS, SNAPS, ROWS, HID, FEAT = 32, 16, 32, 512, 128
GROUPS, STRIPS = 8, 16
DEVS, CHIPS = GROUPS * STRIPS, GROUPS * STRIPS // 2
REGION = 3 * ROWS
PAIRS = ROWS // 2
CHUNK = 4
PAD = 8
MAIN_VMEM = 42 * 1024 * 1024


def dot(a, b):
    return jnp.dot(a, b, preferred_element_type=F32)


def dot_nt(a, b):
    return lax.dot_general(a, b, (((1,), (1,)), ((), ())), preferred_element_type=F32)


def swap_matrix():
    row = lax.broadcasted_iota(jnp.int32, (256, 256), 0)
    col = lax.broadcasted_iota(jnp.int32, (256, 256), 1)
    return jnp.where((row % 16) * 16 + row // 16 == col, 1.0, 0.0).astype(BF16)


def main_kernel(
    initial_hbm, conductivity_hbm, step_count, emit_steps, assign_hbm, sample_hbm,
    w_first, w_second, w_third, w_out,
    gout_hbm, acta_hbm, actb_hbm, hat_hbm, hbt_hbm, xt_hbm, delta_hbm,
    state_a, state_b, kap, quarter, hist, tmp, send, snaps, part, gath,
    raw, w2, pred, resid, acc, pair_in, pieces, delta, act_a, act_b, act_c, hat, hbt, hct, xt, hidc, onehot,
    wf, ws, wt, initial, conductivity, assign, sample_inputs,
    halo_send, halo_recv, part_send, part_recv, gath_send, gath_recv, snap_send, snap_recv,
    pair_send, pair_recv, piece_send, piece_recv, delta_send, delta_recv, twin_send, twin_recv,
    w_sem, raw_sem, own_sem, out_sem, in_sem,
):
    g, s = lax.axis_index("group"), lax.axis_index("strip")
    me = g * STRIPS + s
    core = s % 2
    chip = g * (STRIPS // 2) + s // 2
    twin = me + 1 - 2 * core
    quad = s % 4

    def wrap(i, n):
        return jnp.where(i >= n, i - n, i)

    def each_chip(fn):
        @pl.loop(0, 7)
        def _(i):
            for j in range(9):
                p = wrap(chip + 1 + i * 9 + j, CHIPS)
                fn(p, p * 2 + core)

    def remote(src, dst, send_sem, recv_sem, device):
        return pltpu.make_async_remote_copy(
            src_ref=src, dst_ref=dst, send_sem=send_sem, recv_sem=recv_sem, device_id=device, device_id_type=FLAT
        )

    inputs = [
        pltpu.make_async_copy(a, b, in_sem.at[i])
        for i, (a, b) in enumerate((
            (initial_hbm, initial), (conductivity_hbm, conductivity), (sample_hbm, sample_inputs), (assign_hbm, assign)
        ))
    ]
    for copy in inputs:
        copy.start()
    barrier = pltpu.get_barrier_semaphore()

    def greet(device):
        pl.semaphore_signal(barrier, inc=1, device_id=device, device_id_type=FLAT)

    greet(twin)
    greet(me + 3 - 2 * quad)
    next_quad = ((quad == 0) & (s > 0)) | ((quad == 3) & (s < STRIPS - 1))

    @pl.when(next_quad)
    def _():
        greet(jnp.where(quad == 0, me - 1, me + 1))

    each_chip(lambda p, device: greet(device))

    raw_copies = [
        pltpu.make_async_copy(w_out.at[pl.ds(64 * i, 64)], raw.at[pl.ds(64 * i, 64)], raw_sem.at[i]) for i in range(8)
    ]
    for copy in raw_copies:
        copy.start()
    weight_copies = [
        pltpu.make_async_copy(a, b, w_sem.at[i]) for i, (a, b) in enumerate(((w_first, wf), (w_second, ws), (w_third, wt)))
    ]
    for copy in weight_copies:
        copy.start()

    for copy in inputs:
        copy.wait()
    own_rows, rows_above, rows_below = pl.ds(PAD + ROWS, ROWS), pl.ds(PAD, ROWS), pl.ds(PAD + 2 * ROWS, ROWS)
    for j in range(8):
        state_a[j, own_rows, :] = initial[0, :, j * 128 : (j + 1) * 128]
        kap[j, own_rows, :] = 0.125 * conductivity[0, :, j * 128 : (j + 1) * 128]
        for ref in (state_a, state_b):
            ref[j, 0:PAD, :] = jnp.zeros((PAD, 128), F32)
            ref[j, PAD + REGION :, :] = jnp.zeros((PAD, 128), F32)
    part[quad, 0:4, :] = sample_inputs[...].astype(F32)
    ids = lax.broadcasted_iota(jnp.int32, (DEVS, HID), 0)
    onehot[...] = jnp.transpose(jnp.where(ids == assign[...], 1.0, 0.0)).astype(BF16)
    swap = swap_matrix()

    pl.semaphore_wait(barrier, CHIPS + 1 + jnp.where(next_quad, 1, 0))

    above, below = jnp.where(s > 0, me - 1, me), jnp.where(s < STRIPS - 1, me + 1, me)
    up_copies = [
        remote(ref.at[:, own_rows], ref.at[:, rows_below], halo_send.at[i], halo_recv.at[i], above)
        for i, ref in enumerate((state_a, kap))
    ]
    down_copies = [
        remote(ref.at[:, own_rows], ref.at[:, rows_above], halo_send.at[2 + i], halo_recv.at[2 + i], below)
        for i, ref in enumerate((state_a, kap))
    ]

    @pl.when(s > 0)
    def _():
        for copy in up_copies:
            copy.start()

    @pl.when(s < STRIPS - 1)
    def _():
        for copy in down_copies:
            copy.start()

    for i in range(1, 4):
        remote(part.at[quad], part.at[quad], part_send, part_recv, me - quad + wrap(quad + i, 4)).start()

    def relayout_weights(i, carry):
        for half in range(2):
            k0 = pl.multiple_of((i * 2 + half) * 16, 16)
            x = jnp.concatenate([raw[pl.ds(k0, 16), b * 16 : b * 16 + 16, :].reshape(256, 128) for b in range(2)], axis=1)
            y = dot(swap, x).astype(BF16)
            for b in range(2):
                for r in range(16):
                    row = b * 16 + r
                    w2[row // 2, pl.ds(k0, 16), (row % 2) * 128 : (row % 2) * 128 + 128] = y[
                        r * 16 : r * 16 + 16, b * 128 : b * 128 + 128
                    ]
        return carry

    for i, copy in enumerate(raw_copies):
        copy.wait()
    lax.fori_loop(0, 16, relayout_weights, 0)

    remote(part.at[pl.ds(0, 3)], part.at[pl.ds(0, 3)], part_send, part_recv, twin).wait()
    low = lax.broadcasted_iota(jnp.int32, (8, 128), 0) < 4
    tile = jnp.concatenate(
        [jnp.where(low, part[2 * i], pltpu.roll(part[2 * i + 1], 4, axis=0)) for i in range(2)], axis=0
    )
    mine = g * 4 + s // 4
    gath[mine] = tile.astype(BF16)

    for i in range(1, 32):
        remote(gath.at[mine], gath.at[mine], gath_send, gath_recv, wrap(mine + i, 32) * 4 + quad).start()

    def land(has, copies_in, copies_out, rows):
        @pl.when(has)
        def _():
            for copy in copies_in:
                copy.wait_recv()
            for copy in copies_out:
                copy.wait_send()

        @pl.when(jnp.logical_not(has))
        def _():
            zero = jnp.zeros((8, ROWS, 128), F32)
            state_a[:, rows] = zero
            kap[:, rows] = zero

    land(s > 0, down_copies, up_copies, rows_above)
    land(s < STRIPS - 1, up_copies, down_copies, rows_below)

    @pl.loop(0, 8)
    def _(j):
        quarter[j] = 0.25 * kap[j]

    lane = lax.broadcasted_iota(jnp.int32, (8, 128), 1)
    first_lane, last_lane = lane == 0, lane == 127
    zero_tile = jnp.zeros((8, 128), F32)

    def step(src, dst, first, last, t):
        for tile in range(first, last):
            r = PAD + tile * 8
            here = [src[j, r : r + 8, :] for j in range(8)]
            to_east = [zero_tile] + [pltpu.roll(x, 1, axis=1) for x in here]
            to_west = [pltpu.roll(x, 127, axis=1) for x in here] + [zero_tile]
            for j in range(8):
                w = jnp.where(first_lane, to_east[j], to_east[j + 1])
                e = jnp.where(last_lane, to_west[j + 1], to_west[j])
                beside = (src[j, r - 1 : r + 7, :] + src[j, r + 1 : r + 9, :]) + (e + w)
                rate = kap[j, r : r + 8, :] + quarter[j, r : r + 8, :] * jnp.tanh(here[j])
                new = here[j] + rate * (beside - 4.0 * here[j])
                dst[j, r : r + 8, :] = new
                if ROWS // 8 <= tile < 2 * ROWS // 8:
                    hist[t * 32 + (j * 4 + tile - ROWS // 8)] = new

    for phase in range(4):

        @pl.loop(4 * phase, 4 * phase + 4)
        def _(i):
            step(state_a, state_b, phase, REGION // 8 - phase, 2 * i)
            step(state_b, state_a, phase, REGION // 8 - phase, 2 * i + 1)

    count = step_count[0]
    bases = [jnp.maximum(jnp.minimum(emit_steps[0, k], count) - 1, 0) * 32 for k in range(SNAPS)]

    def pack(c):
        @pl.loop(0, 4)
        def _(i):
            for half in range(2):
                to = i * 2 + half
                for k in range(SNAPS):
                    tmp[to, pl.ds(k, 8, stride=16), :] = hist[bases[k] + (to * 4 + c)]
                for j in range(8):
                    send[to, c * CHUNK + j // 2, :, (j % 2) * 128 : (j % 2) * 128 + 128] = tmp[
                        to, j * 16 : j * 16 + 16, :
                    ].astype(BF16)

    def snap_copy(c, to):
        rows = pl.ds(c * CHUNK, CHUNK)
        return remote(
            send.at[to, rows],
            snaps.at[rows, pl.ds(pl.multiple_of(g * SNAPS, SNAPS), SNAPS), :],
            snap_send,
            snap_recv.at[c],
            to * STRIPS + s,
        )

    for c in range(PAIRS // CHUNK):
        pack(c)
        for i in range(1, GROUPS):
            snap_copy(c, wrap(g + i, GROUPS)).start()

    own = pltpu.make_async_copy(
        send.at[g], snaps.at[:, pl.ds(pl.multiple_of(g * SNAPS, SNAPS), SNAPS), :], own_sem
    )
    own.start()

    for copy in weight_copies:
        copy.wait()
    remote(gath.at[pl.ds(0, 31)], gath.at[pl.ds(0, 31)], gath_send, gath_recv, twin).wait()

    @pl.loop(0, 4)
    def _(m):
        rows = pl.ds(pl.multiple_of(m * 128, 128), 128)
        x = gath[pl.ds(m * 8, 8)].reshape(128, FEAT)
        xt[:, rows] = jnp.transpose(x.astype(F32)).astype(BF16)
        a = jnp.tanh(dot(x, wf[...]))
        act_a[rows, :] = a
        hat[:, rows] = jnp.transpose(a).astype(BF16)
        b = jnp.tanh(dot(a.astype(BF16), ws[...]))
        act_b[rows, :] = b
        hbt[:, rows] = jnp.transpose(b).astype(BF16)
        c = jnp.tanh(dot(b.astype(BF16), wt[...]))
        hct[:, rows] = jnp.transpose(c).astype(BF16)
        hidc[rows, :] = c.astype(BF16)
        for kb in range(4):
            act_c[pl.ds(kb * 32 + m * 8, 8)] = c[:, kb * 128 : kb * 128 + 128].reshape(8, 16, 128)

    outs = [
        pltpu.make_async_copy(a, b, out_sem.at[i])
        for i, (a, b) in enumerate(((act_a, acta_hbm), (act_b, actb_hbm), (hat, hat_hbm), (hbt, hbt_hbm), (xt, xt_hbm)))
    ]
    for copy in outs:
        copy.start()

    @pl.loop(0, PAIRS)
    def _(rp):
        pred[rp] = dot(hidc[...], w2[rp])

    own.wait()
    inverse_root = F32(1.0) / jnp.sqrt(F32(HID))

    def residual_chunk(c):
        remote(snaps.at[pl.ds(0, CHUNK), pl.ds(0, 112), :], snaps.at[pl.ds(0, CHUNK), pl.ds(0, 112), :],
               snap_send, snap_recv.at[c], twin).wait_recv()

        @pl.loop(c * CHUNK, (c + 1) * CHUNK)
        def _(rp):
            resid[rp] = ((pred[rp] - dot(onehot[...], snaps[rp])) * inverse_root).astype(BF16)

    def back_half(c, half, fresh):
        left = jnp.concatenate([resid[c * CHUNK + i] for i in range(CHUNK)], axis=1)
        k0 = pl.multiple_of(half * 256, 256)
        right = jnp.concatenate([w2[c * CHUNK + i, pl.ds(k0, 256), :] for i in range(CHUNK)], axis=1)
        value = dot_nt(left, right)
        for kb in range(2):
            at = pl.ds(half * 64 + kb * 32, 32)
            v = value[:, kb * 128 : kb * 128 + 128].reshape(32, 16, 128)
            acc[at] = v if fresh else acc[at] + v

    residual_chunk(0)
    back_half(0, 1 - core, True)
    back_half(0, core, True)

    @pl.loop(1, 3)
    def _(c):
        residual_chunk(c)
        back_half(c, 1 - core, False)
        back_half(c, core, False)

    residual_chunk(3)
    back_half(3, 1 - core, False)
    theirs = pl.ds((1 - core) * 64, 64)
    to_twin = remote(acc.at[theirs], pair_in, pair_send, pair_recv, twin)
    to_twin.start()
    back_half(3, core, False)
    to_twin.wait_recv()

    @pl.loop(0, 8)
    def _(i):
        at = pl.ds(core * 64 + i * 8, 8)
        acc[at] = acc[at] + pair_in[pl.ds(i * 8, 8)]

    each_chip(
        lambda p, device: remote(acc.at[core * 64 + p], pieces.at[chip], piece_send, piece_recv, device).start()
    )

    pieces[chip] = acc[core * 64 + chip]

    @pl.loop(0, PAIRS)
    def _(rp):
        w2[rp] = dot(hct[...], resid[rp]).astype(BF16)

    remote(pieces.at[pl.ds(0, 63)], pieces.at[pl.ds(0, 63)], piece_send, piece_recv, twin).wait_recv()
    total = pieces[0]
    for i in range(1, CHIPS):
        total = total + pieces[i]
    a = act_c[core * 64 + chip]
    delta[core * 64 + chip] = (total * (1.0 - a * a)).astype(BF16)

    at = core * 64 + chip
    each_chip(lambda p, device: remote(delta.at[at], delta.at[at], delta_send, delta_recv, device).start())

    def relayout_grad(i, carry):
        for half in range(2):
            k0 = pl.multiple_of((i * 2 + half) * 16, 16)
            x = jnp.concatenate(
                [
                    jnp.concatenate(
                        [w2[b * 8 + r // 2, pl.ds(k0, 16), (r % 2) * 128 : (r % 2) * 128 + 128] for r in range(16)], axis=0
                    )
                    for b in range(2)
                ],
                axis=1,
            )
            y = dot(swap, x).astype(BF16)
            for b in range(2):
                raw[pl.ds(k0, 16), b * 16 : b * 16 + 16, :] = y[:, b * 128 : b * 128 + 128].reshape(16, 16, 128)
        return carry

    lax.fori_loop(0, 16, relayout_grad, 0)
    grad_copy = pltpu.make_async_copy(raw, gout_hbm, out_sem.at[5])
    grad_copy.start()

    remote(delta.at[pl.ds(0, 63)], delta.at[pl.ds(0, 63)], delta_send, delta_recv, twin).wait_recv()
    ours = pl.ds(core * 64, 64)
    to_twin2 = remote(delta.at[ours], delta.at[ours], twin_send, twin_recv, twin)
    to_twin2.start()
    to_twin2.wait_recv()
    delta_copy = pltpu.make_async_copy(delta, delta_hbm, out_sem.at[6])
    delta_copy.start()

    remote(send.at[pl.ds(0, 7)], send.at[pl.ds(0, 7)], snap_send, snap_recv.at[0], twin).wait_send()
    to_twin.wait_send()
    remote(pieces.at[pl.ds(0, 63)], pieces.at[pl.ds(0, 63)], piece_send, piece_recv, twin).wait_send()
    remote(delta.at[pl.ds(0, 63)], delta.at[pl.ds(0, 63)], delta_send, delta_recv, twin).wait_send()
    to_twin2.wait_send()
    for copy in outs:
        copy.wait()
    grad_copy.wait()
    delta_copy.wait()


def final_kernel(
    gout_in, act_a, act_b, hat, hbt, xt, delta, ws_in, wt_in, g1_out, g2_out, g3_out, gout_out, ws, wt, g1, g2, g3, in_sem, out_sem
):
    loads = [pltpu.make_async_copy(a, b, in_sem.at[i]) for i, (a, b) in enumerate(((wt_in, wt), (ws_in, ws)))]
    for copy in loads:
        copy.start()
    to_gout = pltpu.make_async_copy(gout_in, gout_out, out_sem.at[3])
    to_gout.start()
    dc = jnp.concatenate([delta[i * 32 : i * 32 + 32].reshape(HID, 128) for i in range(4)], axis=1)
    g3[...] = dot(hbt[...], dc)
    to_g3 = pltpu.make_async_copy(g3, g3_out, out_sem.at[0])
    to_g3.start()
    loads[0].wait()
    db = (dot_nt(dc, wt[...]) * (1.0 - act_b[...] * act_b[...])).astype(BF16)
    g2[...] = dot(hat[...], db)
    to_g2 = pltpu.make_async_copy(g2, g2_out, out_sem.at[1])
    to_g2.start()
    loads[1].wait()
    da = (dot_nt(db, ws[...]) * (1.0 - act_a[...] * act_a[...])).astype(BF16)
    g1[...] = dot(xt[...], da)
    to_g1 = pltpu.make_async_copy(g1, g1_out, out_sem.at[2])
    to_g1.start()
    for copy in (to_gout, to_g3, to_g2, to_g1):
        copy.wait()


def per_device(initial, conductivity, step_count, emit_steps, assign, sample_inputs, w_first, w_second, w_third, w_out):
    vmem, smem = pl.BlockSpec(memory_space=pltpu.VMEM), pl.BlockSpec(memory_space=pltpu.SMEM)
    hbm = pl.BlockSpec(memory_space=pl.ANY)
    far = pl.BlockSpec(memory_space=pltpu.HBM)
    shape = jax.ShapeDtypeStruct
    dma = pltpu.SemaphoreType.DMA
    pin = lambda x: pltpu.with_memory_space_constraint(x, pltpu.HBM)
    mats = (
        shape((HID, HID), F32), shape((HID, HID), F32), shape((HID, HID), BF16), shape((HID, HID), BF16),
        shape((FEAT, HID), BF16), shape((DEVS, 16, 128), BF16),
    )
    gout, *kept = pl.pallas_call(
        main_kernel,
        out_shape=(shape((HID, ROWS, 128), BF16),) + mats,
        in_specs=[far, far, smem, smem, far, far, far, far, far, far],
        out_specs=[hbm] * 7,
        scratch_shapes=[
            *[pltpu.VMEM((8, REGION + 2 * PAD, 128), F32)] * 4,
            pltpu.VMEM((STEPS * ROWS, 8, 128), F32),
            pltpu.VMEM((GROUPS, 128, 128), F32),
            pltpu.VMEM((GROUPS, PAIRS, SNAPS, 256), BF16),
            pltpu.VMEM((PAIRS, DEVS, 256), BF16),
            pltpu.VMEM((4, 8, 128), F32),
            pltpu.VMEM((32, 16, 128), BF16),
            pltpu.VMEM((HID, ROWS, 128), BF16),
            pltpu.VMEM((PAIRS, HID, 256), BF16),
            pltpu.VMEM((PAIRS, HID, 256), F32),
            pltpu.VMEM((PAIRS, HID, 256), BF16),
            pltpu.VMEM((DEVS, 16, 128), F32),
            pltpu.VMEM((64, 16, 128), F32),
            pltpu.VMEM((CHIPS, 16, 128), F32),
            pltpu.VMEM((DEVS, 16, 128), BF16),
            pltpu.VMEM((HID, HID), F32), pltpu.VMEM((HID, HID), F32), pltpu.VMEM((DEVS, 16, 128), F32),
            pltpu.VMEM((HID, HID), BF16), pltpu.VMEM((HID, HID), BF16), pltpu.VMEM((HID, HID), BF16),
            pltpu.VMEM((FEAT, HID), BF16), pltpu.VMEM((HID, HID), BF16), pltpu.VMEM((HID, DEVS), BF16),
            pltpu.VMEM((FEAT, HID), BF16), pltpu.VMEM((HID, HID), BF16), pltpu.VMEM((HID, HID), BF16),
            pltpu.VMEM((1, ROWS, 1024), F32), pltpu.VMEM((1, ROWS, 1024), F32), pltpu.VMEM((1, HID), jnp.int32), pltpu.VMEM((4, FEAT), BF16),
            dma((4,)), dma((4,)), dma, dma, dma, dma, dma, dma((4,)),
            dma, dma, dma, dma, dma, dma, dma, dma,
            dma((3,)), dma((8,)), dma, dma((7,)), dma((4,)),
        ],
        compiler_params=pltpu.CompilerParams(
            collective_id=0, has_side_effects=True, vmem_limit_bytes=MAIN_VMEM
        ),
        name="solve_and_reduce",
    )(
        pin(initial), pin(conductivity), step_count, pin(emit_steps), pin(assign.reshape(1, HID)), pin(sample_inputs),
        pin(w_first), pin(w_second), pin(w_third), pin(w_out),
    )
    outs = pl.pallas_call(
        final_kernel,
        out_shape=(shape((FEAT, HID), F32), shape((HID, HID), F32), shape((HID, HID), F32), shape((HID, ROWS, 128), BF16)),
        in_specs=[hbm] + [vmem] * 6 + [far] * 2,
        out_specs=[hbm] * 4,
        scratch_shapes=[
            pltpu.VMEM((HID, HID), BF16), pltpu.VMEM((HID, HID), BF16),
            pltpu.VMEM((FEAT, HID), F32), pltpu.VMEM((HID, HID), F32), pltpu.VMEM((HID, HID), F32),
            dma((2,)), dma((4,)),
        ],
        name="outputs",
        compiler_params=pltpu.CompilerParams(vmem_limit_bytes=12 * 1024 * 1024),
    )(gout, *kept, pin(w_second), pin(w_third))
    return tuple(outs)


def solution(mesh):
    placed = (
        P("group", "strip", None), P("group", "strip", None), P("group"), P("group", None), P(),
        P(("group", "strip"), None), P(), P(), P(), P(None, "strip", "group"),
    )
    return jax.shard_map(
        per_device, mesh=mesh, in_specs=placed, out_specs=(P(), P(), P(), P(None, "strip", "group")), check_vma=False
    )
```

time: 71 us -> 64.7 us (0.911)
  Pallas kernels: 69.6 us -> 63.3 us
    pallas_call x1, Pallas kernels: 7.47 us -> 3.96 us  [per_device(): pl.pallas_call(final_kernel, out_shape=(shape((FEAT, HID), F32), shape((H...]
    pallas_call x1, Pallas kernels: 62.1 us -> 59.3 us  [per_device(): pl.pallas_call(main_kernel, out_shape=(shape((HID, ROWS, 128), BF16),) +...]
where the time goes in v2:
time: 64.7 us; the launch traced here: 64.6 us
  Pallas kernels  63.3 us (98%)
  between operations  1.29 us (2%)
    pallas_call x1, Pallas kernels, per_device(): pl.pallas_call(main_kernel, out_shape=(shape((HID, ROWS, 128), BF16),) +...  59.3 us
    pallas_call x1, Pallas kernels, per_device(): pl.pallas_call(final_kernel, out_shape=(shape((FEAT, HID), F32), shape((H...  3.96 us

profile of v2, /device:TPU:1, one launch (start us, length us, event | category | flops | bytes accessed | tf_op | source)
XLA Modules:
  0.0 64.6 jit_solution(10682334520141915902)
XLA Ops:
  1.3 59.3 %solve_and_reduce.1 = (bf16[512,32,128]{2,1,0:T(8,128)(2,1)S(1)}, f32[512,512]{1,0:T(8,128)S(1)}, f32[512,512]{1,0:T(8,128)S(1)}, bf16[512,512]{1,0:T(8,128)(2,1...) custom-call(f32[1,32,1024]{2,1,0:T(8,128)} %initial_hbm.1, ...), custom_call_target="tpu_custom_call" | custom-call | tf_op jit(solution)/shard_map/solve_and_reduce/pallas_call | solution.py:424
  60.6 4.0 %outputs.1 = (f32[128,512]{1,0:T(8,128)}, f32[512,512]{1,0:T(8,128)}, f32[512,512]{1,0:T(8,128)}, bf16[512,32,128]{2,1,0:T(8,128)(2,1)}) custom-call(bf16[512,32,128]{2,1,0:T(8,128)(2,1)S(1)} %get-tuple-element.11.gout_in, f32[512,512]{1,0:T(8,128)S(1)} %get-tuple-element.12.act_a, f32[512,512]{1,0:T(8,128)S(1)} %get-tuple-element.13.act_b, ...), custom_call_target="tpu_custom_call" | custom-call | tf_op jit(solution)/shard_map/outputs/pallas_call | solution.py:462

commit v3 on v2

--- a/solution.py
+++ b/solution.py
@@ -34,13 +34,13 @@
 def main_kernel(
     initial_hbm, conductivity_hbm, step_count, emit_steps, assign_hbm, sample_hbm,
     w_first, w_second, w_third, w_out,
-    gout_hbm, acta_hbm, actb_hbm, hat_hbm, hbt_hbm, xt_hbm, delta_hbm,
+    gout, act_a, act_b, hat, hbt, xt, delta_out,
     state_a, state_b, kap, quarter, hist, tmp, send, snaps, part, gath,
-    raw, w2, pred, resid, acc, pair_in, pieces, delta, act_a, act_b, act_c, hat, hbt, hct, xt, hidc, onehot,
+    raw, w2, pred, resid, acc, pair_in, pieces, mine_bf, delta, act_c, hct, hidc, onehot,
     wf, ws, wt, initial, conductivity, assign, sample_inputs,
     halo_send, halo_recv, part_send, part_recv, gath_send, gath_recv, snap_send, snap_recv,
     pair_send, pair_recv, piece_send, piece_recv, delta_send, delta_recv, twin_send, twin_recv,
-    w_sem, raw_sem, own_sem, out_sem, in_sem,
+    w_sem, raw_sem, own_sem, in_sem,
 ):
     g, s = lax.axis_index("group"), lax.axis_index("strip")
     me = g * STRIPS + s
@@ -269,13 +269,6 @@
         for kb in range(4):
             act_c[pl.ds(kb * 32 + m * 8, 8)] = c[:, kb * 128 : kb * 128 + 128].reshape(8, 16, 128)
 
-    outs = [
-        pltpu.make_async_copy(a, b, out_sem.at[i])
-        for i, (a, b) in enumerate(((act_a, acta_hbm), (act_b, actb_hbm), (hat, hat_hbm), (hbt, hbt_hbm), (xt, xt_hbm)))
-    ]
-    for copy in outs:
-        copy.start()
-
     @pl.loop(0, PAIRS)
     def _(rp):
         pred[rp] = dot(hidc[...], w2[rp])
@@ -287,9 +280,11 @@
         remote(snaps.at[pl.ds(0, CHUNK), pl.ds(0, 112), :], snaps.at[pl.ds(0, CHUNK), pl.ds(0, 112), :],
                snap_send, snap_recv.at[c], twin).wait_recv()
 
-        @pl.loop(c * CHUNK, (c + 1) * CHUNK)
-        def _(rp):
-            resid[rp] = ((pred[rp] - dot(onehot[...], snaps[rp])) * inverse_root).astype(BF16)
+        @pl.loop(0, CHUNK // 2)
+        def _(i):
+            for half in range(2):
+                rp = c * CHUNK + 2 * i + half
+                resid[rp] = ((pred[rp] - dot(onehot[...], snaps[rp])) * inverse_root).astype(BF16)
 
     def back_half(c, half, fresh):
         left = jnp.concatenate([resid[c * CHUNK + i] for i in range(CHUNK)], axis=1)
@@ -303,41 +298,42 @@
 
     residual_chunk(0)
     back_half(0, 1 - core, True)
-    back_half(0, core, True)
-
-    @pl.loop(1, 3)
+
+    @pl.loop(1, PAIRS // CHUNK)
     def _(c):
         residual_chunk(c)
         back_half(c, 1 - core, False)
-        back_half(c, core, False)
-
-    residual_chunk(3)
-    back_half(3, 1 - core, False)
+
     theirs = pl.ds((1 - core) * 64, 64)
     to_twin = remote(acc.at[theirs], pair_in, pair_send, pair_recv, twin)
     to_twin.start()
-    back_half(3, core, False)
+    back_half(0, core, True)
+
+    @pl.loop(1, PAIRS // CHUNK)
+    def _(c):
+        back_half(c, core, False)
+
     to_twin.wait_recv()
 
     @pl.loop(0, 8)
     def _(i):
-        at = pl.ds(core * 64 + i * 8, 8)
-        acc[at] = acc[at] + pair_in[pl.ds(i * 8, 8)]
+        at = pl.ds(i * 8, 8)
+        mine_bf[at] = (acc[pl.ds(core * 64 + i * 8, 8)] + pair_in[at]).astype(BF16)
 
     each_chip(
-        lambda p, device: remote(acc.at[core * 64 + p], pieces.at[chip], piece_send, piece_recv, device).start()
-    )
-
-    pieces[chip] = acc[core * 64 + chip]
+        lambda p, device: remote(mine_bf.at[p], pieces.at[chip], piece_send, piece_recv, device).start()
+    )
+
+    pieces[chip] = mine_bf[chip]
 
     @pl.loop(0, PAIRS)
     def _(rp):
         w2[rp] = dot(hct[...], resid[rp]).astype(BF16)
 
     remote(pieces.at[pl.ds(0, 63)], pieces.at[pl.ds(0, 63)], piece_send, piece_recv, twin).wait_recv()
-    total = pieces[0]
+    total = pieces[0].astype(F32)
     for i in range(1, CHIPS):
-        total = total + pieces[i]
+        total = total + pieces[i].astype(F32)
     a = act_c[core * 64 + chip]
     delta[core * 64 + chip] = (total * (1.0 - a * a)).astype(BF16)
 
@@ -358,30 +354,23 @@
             )
             y = dot(swap, x).astype(BF16)
             for b in range(2):
-                raw[pl.ds(k0, 16), b * 16 : b * 16 + 16, :] = y[:, b * 128 : b * 128 + 128].reshape(16, 16, 128)
+                gout[pl.ds(k0, 16), b * 16 : b * 16 + 16, :] = y[:, b * 128 : b * 128 + 128].reshape(16, 16, 128)
         return carry
 
     lax.fori_loop(0, 16, relayout_grad, 0)
-    grad_copy = pltpu.make_async_copy(raw, gout_hbm, out_sem.at[5])
-    grad_copy.start()
 
     remote(delta.at[pl.ds(0, 63)], delta.at[pl.ds(0, 63)], delta_send, delta_recv, twin).wait_recv()
     ours = pl.ds(core * 64, 64)
     to_twin2 = remote(delta.at[ours], delta.at[ours], twin_send, twin_recv, twin)
     to_twin2.start()
     to_twin2.wait_recv()
-    delta_copy = pltpu.make_async_copy(delta, delta_hbm, out_sem.at[6])
-    delta_copy.start()
+    delta_out[...] = delta[...]
 
     remote(send.at[pl.ds(0, 7)], send.at[pl.ds(0, 7)], snap_send, snap_recv.at[0], twin).wait_send()
     to_twin.wait_send()
     remote(pieces.at[pl.ds(0, 63)], pieces.at[pl.ds(0, 63)], piece_send, piece_recv, twin).wait_send()
     remote(delta.at[pl.ds(0, 63)], delta.at[pl.ds(0, 63)], delta_send, delta_recv, twin).wait_send()
     to_twin2.wait_send()
-    for copy in outs:
-        copy.wait()
-    grad_copy.wait()
-    delta_copy.wait()
 
 
 def final_kernel(
@@ -425,7 +414,7 @@
         main_kernel,
         out_shape=(shape((HID, ROWS, 128), BF16),) + mats,
         in_specs=[far, far, smem, smem, far, far, far, far, far, far],
-        out_specs=[hbm] * 7,
+        out_specs=[vmem] * 7,
         scratch_shapes=[
             *[pltpu.VMEM((8, REGION + 2 * PAD, 128), F32)] * 4,
             pltpu.VMEM((STEPS * ROWS, 8, 128), F32),
@@ -440,16 +429,15 @@
             pltpu.VMEM((PAIRS, HID, 256), BF16),
             pltpu.VMEM((DEVS, 16, 128), F32),
             pltpu.VMEM((64, 16, 128), F32),
-            pltpu.VMEM((CHIPS, 16, 128), F32),
+            pltpu.VMEM((CHIPS, 16, 128), BF16), pltpu.VMEM((CHIPS, 16, 128), BF16),
             pltpu.VMEM((DEVS, 16, 128), BF16),
-            pltpu.VMEM((HID, HID), F32), pltpu.VMEM((HID, HID), F32), pltpu.VMEM((DEVS, 16, 128), F32),
-            pltpu.VMEM((HID, HID), BF16), pltpu.VMEM((HID, HID), BF16), pltpu.VMEM((HID, HID), BF16),
-            pltpu.VMEM((FEAT, HID), BF16), pltpu.VMEM((HID, HID), BF16), pltpu.VMEM((HID, DEVS), BF16),
+            pltpu.VMEM((DEVS, 16, 128), F32), pltpu.VMEM((HID, HID), BF16),
+            pltpu.VMEM((HID, HID), BF16), pltpu.VMEM((HID, DEVS), BF16),
             pltpu.VMEM((FEAT, HID), BF16), pltpu.VMEM((HID, HID), BF16), pltpu.VMEM((HID, HID), BF16),
             pltpu.VMEM((1, ROWS, 1024), F32), pltpu.VMEM((1, ROWS, 1024), F32), pltpu.VMEM((1, HID), jnp.int32), pltpu.VMEM((4, FEAT), BF16),
             dma((4,)), dma((4,)), dma, dma, dma, dma, dma, dma((4,)),
             dma, dma, dma, dma, dma, dma, dma, dma,
-            dma((3,)), dma((8,)), dma, dma((7,)), dma((4,)),
+            dma((3,)), dma((8,)), dma, dma((4,)),
         ],
         compiler_params=pltpu.CompilerParams(
             collective_id=0, has_side_effects=True, vmem_limit_bytes=MAIN_VMEM

time: 64.7 us -> 61.3 us (0.947)
  Pallas kernels: 63.3 us -> 59.8 us
    pallas_call x1, Pallas kernels: 59.3 us -> 55.9 us  [per_device(): pl.pallas_call(main_kernel, out_shape=(shape((HID, ROWS, 128), BF16),) +...]
where the time goes in v3:
time: 61.3 us; the launch traced here: 61.1 us
  Pallas kernels  59.8 us (98%)
  between operations  1.29 us (2%)
    pallas_call x1, Pallas kernels, per_device(): pl.pallas_call(main_kernel, out_shape=(shape((HID, ROWS, 128), BF16),) +...  55.9 us
    pallas_call x1, Pallas kernels, per_device(): pl.pallas_call(final_kernel, out_shape=(shape((FEAT, HID), F32), shape((H...  3.96 us

profile of v3, /device:TPU:1, one launch (start us, length us, event | category | flops | bytes accessed | tf_op | source)
XLA Modules:
  0.0 61.1 jit_solution(16292994658882961086)
XLA Ops:
  1.3 55.9 %solve_and_reduce.1 = (bf16[512,32,128]{2,1,0:T(8,128)(2,1)S(1)}, f32[512,512]{1,0:T(8,128)S(1)}, f32[512,512]{1,0:T(8,128)S(1)}, bf16[512,512]{1,0:T(8,128)(2,1...) custom-call(f32[1,32,1024]{2,1,0:T(8,128)} %initial_hbm.1, ...), custom_call_target="tpu_custom_call" | custom-call | tf_op jit(solution)/shard_map/solve_and_reduce/pallas_call | solution.py:413
  57.2 4.0 %outputs.1 = (f32[128,512]{1,0:T(8,128)}, f32[512,512]{1,0:T(8,128)}, f32[512,512]{1,0:T(8,128)}, bf16[512,32,128]{2,1,0:T(8,128)(2,1)}) custom-call(bf16[512,32,128]{2,1,0:T(8,128)(2,1)S(1)} %get-tuple-element.11.gout_in, f32[512,512]{1,0:T(8,128)S(1)} %get-tuple-element.12.act_a, f32[512,512]{1,0:T(8,128)S(1)} %get-tuple-element.13.act_b, ...), custom_call_target="tpu_custom_call" | custom-call | tf_op jit(solution)/shard_map/outputs/pallas_call | solution.py:450

commit v4 on v3

--- a/solution.py
+++ b/solution.py
@@ -74,18 +74,28 @@
         copy.start()
     barrier = pltpu.get_barrier_semaphore()
 
+    z, x_lo, x_hi, y = (s // 2) % 4, s // 8, g % 2, g // 2
+    doubling = [
+        me + 2 * (3 - 2 * z),
+        me + 8 * (1 - 2 * x_lo),
+        me + 16 * (1 - 2 * x_hi) + 8 * (1 - 2 * x_lo),
+        me + 32 * (1 - 2 * (y % 2)),
+        me + 32 * (3 - 2 * y),
+    ]
+
     def greet(device):
         pl.semaphore_signal(barrier, inc=1, device_id=device, device_id_type=FLAT)
 
     greet(twin)
     greet(me + 3 - 2 * quad)
+    greet(me + 2 - 4 * (quad // 2))
+    for device in doubling:
+        greet(device)
     next_quad = ((quad == 0) & (s > 0)) | ((quad == 3) & (s < STRIPS - 1))
 
     @pl.when(next_quad)
     def _():
         greet(jnp.where(quad == 0, me - 1, me + 1))
-
-    each_chip(lambda p, device: greet(device))
 
     raw_copies = [
         pltpu.make_async_copy(w_out.at[pl.ds(64 * i, 64)], raw.at[pl.ds(64 * i, 64)], raw_sem.at[i]) for i in range(8)
@@ -112,7 +122,7 @@
     onehot[...] = jnp.transpose(jnp.where(ids == assign[...], 1.0, 0.0)).astype(BF16)
     swap = swap_matrix()
 
-    pl.semaphore_wait(barrier, CHIPS + 1 + jnp.where(next_quad, 1, 0))
+    pl.semaphore_wait(barrier, 8 + jnp.where(next_quad, 1, 0))
 
     above, below = jnp.where(s > 0, me - 1, me), jnp.where(s < STRIPS - 1, me + 1, me)
     up_copies = [
@@ -152,8 +162,7 @@
 
     for i, copy in enumerate(raw_copies):
         copy.wait()
-    lax.fori_loop(0, 16, relayout_weights, 0)
-
+    lax.fori_loop(0, 8, relayout_weights, 0)
     remote(part.at[pl.ds(0, 3)], part.at[pl.ds(0, 3)], part_send, part_recv, twin).wait()
     low = lax.broadcasted_iota(jnp.int32, (8, 128), 0) < 4
     tile = jnp.concatenate(
@@ -162,8 +171,15 @@
     mine = g * 4 + s // 4
     gath[mine] = tile.astype(BF16)
 
-    for i in range(1, 32):
-        remote(gath.at[mine], gath.at[mine], gath_send, gath_recv, wrap(mine + i, 32) * 4 + quad).start()
+
+    def tiles(stage):
+        held = pl.ds(mine // 2**stage * 2**stage, 2**stage)
+        return remote(gath.at[held], gath.at[held], gath_send.at[stage], gath_recv.at[stage], doubling[stage])
+
+    tiles(0).start()
+    lax.fori_loop(8, 16, relayout_weights, 0)
+    tiles(0).wait()
+    tiles(1).start()
 
     def land(has, copies_in, copies_out, rows):
         @pl.when(has)
@@ -213,6 +229,10 @@
             step(state_a, state_b, phase, REGION // 8 - phase, 2 * i)
             step(state_b, state_a, phase, REGION // 8 - phase, 2 * i + 1)
 
+        tiles(phase + 1).wait()
+        if phase < 3:
+            tiles(phase + 2).start()
+
     count = step_count[0]
     bases = [jnp.maximum(jnp.minimum(emit_steps[0, k], count) - 1, 0) * 32 for k in range(SNAPS)]
 
@@ -250,7 +270,6 @@
 
     for copy in weight_copies:
         copy.wait()
-    remote(gath.at[pl.ds(0, 31)], gath.at[pl.ds(0, 31)], gath_send, gath_recv, twin).wait()
 
     @pl.loop(0, 4)
     def _(m):
@@ -435,7 +454,7 @@
             pltpu.VMEM((HID, HID), BF16), pltpu.VMEM((HID, DEVS), BF16),
             pltpu.VMEM((FEAT, HID), BF16), pltpu.VMEM((HID, HID), BF16), pltpu.VMEM((HID, HID), BF16),
             pltpu.VMEM((1, ROWS, 1024), F32), pltpu.VMEM((1, ROWS, 1024), F32), pltpu.VMEM((1, HID), jnp.int32), pltpu.VMEM((4, FEAT), BF16),
-            dma((4,)), dma((4,)), dma, dma, dma, dma, dma, dma((4,)),
+            dma((4,)), dma((4,)), dma, dma, dma((5,)), dma((5,)), dma, dma((4,)),
             dma, dma, dma, dma, dma, dma, dma, dma,
             dma((3,)), dma((8,)), dma, dma((4,)),
         ],

time: 61.3 us -> 68.6 us (1.12)
  Pallas kernels: 59.8 us -> 67.1 us
    pallas_call x1, Pallas kernels: 55.9 us -> 63.1 us  [per_device(): pl.pallas_call(main_kernel, out_shape=(shape((HID, ROWS, 128), BF16),) +...]
where the time goes in v4:
time: 68.6 us; the launch traced here: 68.4 us
  Pallas kernels  67.1 us (98%)
  between operations  1.29 us (2%)
    pallas_call x1, Pallas kernels, per_device(): pl.pallas_call(main_kernel, out_shape=(shape((HID, ROWS, 128), BF16),) +...  63.1 us
    pallas_call x1, Pallas kernels, per_device(): pl.pallas_call(final_kernel, out_shape=(shape((FEAT, HID), F32), shape((H...  3.96 us

profile of v4, /device:TPU:1, one launch (start us, length us, event | category | flops | bytes accessed | tf_op | source)
XLA Modules:
  0.0 68.4 jit_solution(2779039257692545292)
XLA Ops:
  1.3 63.1 %solve_and_reduce.1 = (bf16[512,32,128]{2,1,0:T(8,128)(2,1)S(1)}, f32[512,512]{1,0:T(8,128)S(1)}, f32[512,512]{1,0:T(8,128)S(1)}, bf16[512,512]{1,0:T(8,128)(2,1...) custom-call(f32[1,32,1024]{2,1,0:T(8,128)} %initial_hbm.1, ...), custom_call_target="tpu_custom_call" | custom-call | tf_op jit(solution)/shard_map/solve_and_reduce/pallas_call | solution.py:432
  64.4 4.0 %outputs.1 = (f32[128,512]{1,0:T(8,128)}, f32[512,512]{1,0:T(8,128)}, f32[512,512]{1,0:T(8,128)}, bf16[512,32,128]{2,1,0:T(8,128)(2,1)}) custom-call(bf16[512,32,128]{2,1,0:T(8,128)(2,1)S(1)} %get-tuple-element.11.gout_in, f32[512,512]{1,0:T(8,128)S(1)} %get-tuple-element.12.act_a, f32[512,512]{1,0:T(8,128)S(1)} %get-tuple-element.13.act_b, ...), custom_call_target="tpu_custom_call" | custom-call | tf_op jit(solution)/shard_map/outputs/pallas_call | solution.py:469

commit v5 on v4

--- a/solution.py
+++ b/solution.py
@@ -40,7 +40,7 @@
     wf, ws, wt, initial, conductivity, assign, sample_inputs,
     halo_send, halo_recv, part_send, part_recv, gath_send, gath_recv, snap_send, snap_recv,
     pair_send, pair_recv, piece_send, piece_recv, delta_send, delta_recv, twin_send, twin_recv,
-    w_sem, raw_sem, own_sem, in_sem,
+    w_sem, raw_sem, own_sem, in_sem, known,
 ):
     g, s = lax.axis_index("group"), lax.axis_index("strip")
     me = g * STRIPS + s
@@ -162,7 +162,13 @@
 
     for i, copy in enumerate(raw_copies):
         copy.wait()
-    lax.fori_loop(0, 8, relayout_weights, 0)
+    def tell(stage):
+        pl.semaphore_signal(known.at[stage], inc=1, device_id=doubling[stage], device_id_type=FLAT)
+
+    def hear(stage):
+        pl.semaphore_wait(known.at[stage], 1)
+
+    lax.fori_loop(0, 7, relayout_weights, 0)
     remote(part.at[pl.ds(0, 3)], part.at[pl.ds(0, 3)], part_send, part_recv, twin).wait()
     low = lax.broadcasted_iota(jnp.int32, (8, 128), 0) < 4
     tile = jnp.concatenate(
@@ -170,16 +176,11 @@
     )
     mine = g * 4 + s // 4
     gath[mine] = tile.astype(BF16)
-
-
-    def tiles(stage):
-        held = pl.ds(mine // 2**stage * 2**stage, 2**stage)
-        return remote(gath.at[held], gath.at[held], gath_send.at[stage], gath_recv.at[stage], doubling[stage])
-
-    tiles(0).start()
-    lax.fori_loop(8, 16, relayout_weights, 0)
-    tiles(0).wait()
-    tiles(1).start()
+    for stage in range(3):
+        tell(stage)
+        lax.fori_loop(7 + 3 * stage, 10 + 3 * stage, relayout_weights, 0)
+        hear(stage)
+    tell(3)
 
     def land(has, copies_in, copies_out, rows):
         @pl.when(has)
@@ -197,6 +198,9 @@
 
     land(s > 0, down_copies, up_copies, rows_above)
     land(s < STRIPS - 1, up_copies, down_copies, rows_below)
+
+    hear(3)
+    tell(4)
 
     @pl.loop(0, 8)
     def _(j):
@@ -229,9 +233,10 @@
             step(state_a, state_b, phase, REGION // 8 - phase, 2 * i)
             step(state_b, state_a, phase, REGION // 8 - phase, 2 * i + 1)
 
-        tiles(phase + 1).wait()
-        if phase < 3:
-            tiles(phase + 2).start()
+        if phase == 0:
+            hear(4)
+            for i in range(1, 32):
+                remote(gath.at[mine], gath.at[mine], gath_send, gath_recv, wrap(mine + i, 32) * 4 + quad).start()
 
     count = step_count[0]
     bases = [jnp.maximum(jnp.minimum(emit_steps[0, k], count) - 1, 0) * 32 for k in range(SNAPS)]
@@ -270,6 +275,7 @@
 
     for copy in weight_copies:
         copy.wait()
+    remote(gath.at[pl.ds(0, 31)], gath.at[pl.ds(0, 31)], gath_send, gath_recv, twin).wait()
 
     @pl.loop(0, 4)
     def _(m):
@@ -454,9 +460,9 @@
             pltpu.VMEM((HID, HID), BF16), pltpu.VMEM((HID, DEVS), BF16),
             pltpu.VMEM((FEAT, HID), BF16), pltpu.VMEM((HID, HID), BF16), pltpu.VMEM((HID, HID), BF16),
             pltpu.VMEM((1, ROWS, 1024), F32), pltpu.VMEM((1, ROWS, 1024), F32), pltpu.VMEM((1, HID), jnp.int32), pltpu.VMEM((4, FEAT), BF16),
-            dma((4,)), dma((4,)), dma, dma, dma((5,)), dma((5,)), dma, dma((4,)),
+            dma((4,)), dma((4,)), dma, dma, dma, dma, dma, dma((4,)),
             dma, dma, dma, dma, dma, dma, dma, dma,
-            dma((3,)), dma((8,)), dma, dma((4,)),
+            dma((3,)), dma((8,)), dma, dma((4,)), pltpu.SemaphoreType.REGULAR((5,)),
         ],
         compiler_params=pltpu.CompilerParams(
             collective_id=0, has_side_effects=True, vmem_limit_bytes=MAIN_VMEM

time: 68.6 us -> 62.9 us (0.917)
  Pallas kernels: 67.1 us -> 61.4 us
    pallas_call x1, Pallas kernels: 63.1 us -> 57.4 us  [per_device(): pl.pallas_call(main_kernel, out_shape=(shape((HID, ROWS, 128), BF16),) +...]
where the time goes in v5:
time: 62.9 us; the launch traced here: 62.7 us
  Pallas kernels  61.4 us (98%)
  between operations  1.29 us (2%)
    pallas_call x1, Pallas kernels, per_device(): pl.pallas_call(main_kernel, out_shape=(shape((HID, ROWS, 128), BF16),) +...  57.4 us
    pallas_call x1, Pallas kernels, per_device(): pl.pallas_call(final_kernel, out_shape=(shape((FEAT, HID), F32), shape((H...  3.97 us

profile of v5, /device:TPU:1, one launch (start us, length us, event | category | flops | bytes accessed | tf_op | source)
XLA Modules:
  0.0 62.7 jit_solution(8756908556744218066)
XLA Ops:
  1.3 57.4 %solve_and_reduce.1 = (bf16[512,32,128]{2,1,0:T(8,128)(2,1)S(1)}, f32[512,512]{1,0:T(8,128)S(1)}, f32[512,512]{1,0:T(8,128)S(1)}, bf16[512,512]{1,0:T(8,128)(2,1...) custom-call(f32[1,32,1024]{2,1,0:T(8,128)} %initial_hbm.1, ...), custom_call_target="tpu_custom_call" | custom-call | tf_op jit(solution)/shard_map/solve_and_reduce/pallas_call | solution.py:438
  58.7 4.0 %outputs.1 = (f32[128,512]{1,0:T(8,128)}, f32[512,512]{1,0:T(8,128)}, f32[512,512]{1,0:T(8,128)}, bf16[512,32,128]{2,1,0:T(8,128)(2,1)}) custom-call(bf16[512,32,128]{2,1,0:T(8,128)(2,1)S(1)} %get-tuple-element.11.gout_in, f32[512,512]{1,0:T(8,128)S(1)} %get-tuple-element.12.act_a, f32[512,512]{1,0:T(8,128)S(1)} %get-tuple-element.13.act_b, ...), custom_call_target="tpu_custom_call" | custom-call | tf_op jit(solution)/shard_map/outputs/pallas_call | solution.py:475

commit v6 on v3

--- a/solution.py
+++ b/solution.py
@@ -36,11 +36,11 @@
     w_first, w_second, w_third, w_out,
     gout, act_a, act_b, hat, hbt, xt, delta_out,
     state_a, state_b, kap, quarter, hist, tmp, send, snaps, part, gath,
-    raw, w2, pred, resid, acc, pair_in, pieces, mine_bf, delta, act_c, hct, hidc, onehot,
+    raw, w2, pred, resid, acc, pair_in, pair_out, pieces, mine_bf, delta, act_c, hct, hidc, onehot,
     wf, ws, wt, initial, conductivity, assign, sample_inputs,
     halo_send, halo_recv, part_send, part_recv, gath_send, gath_recv, snap_send, snap_recv,
     pair_send, pair_recv, piece_send, piece_recv, delta_send, delta_recv, twin_send, twin_recv,
-    w_sem, raw_sem, own_sem, in_sem,
+    w_sem, raw_sem, own_sem, in_sem, known,
 ):
     g, s = lax.axis_index("group"), lax.axis_index("strip")
     me = g * STRIPS + s
@@ -74,18 +74,10 @@
         copy.start()
     barrier = pltpu.get_barrier_semaphore()
 
-    def greet(device):
-        pl.semaphore_signal(barrier, inc=1, device_id=device, device_id_type=FLAT)
-
-    greet(twin)
-    greet(me + 3 - 2 * quad)
-    next_quad = ((quad == 0) & (s > 0)) | ((quad == 3) & (s < STRIPS - 1))
-
-    @pl.when(next_quad)
-    def _():
-        greet(jnp.where(quad == 0, me - 1, me + 1))
-
-    each_chip(lambda p, device: greet(device))
+    for i in range(1, STRIPS):
+        pl.semaphore_signal(barrier, inc=1, device_id=g * STRIPS + wrap(s + i, STRIPS), device_id_type=FLAT)
+    for i in range(1, GROUPS):
+        pl.semaphore_signal(barrier, inc=1, device_id=wrap(g + i, GROUPS) * STRIPS + s, device_id_type=FLAT)
 
     raw_copies = [
         pltpu.make_async_copy(w_out.at[pl.ds(64 * i, 64)], raw.at[pl.ds(64 * i, 64)], raw_sem.at[i]) for i in range(8)
@@ -112,7 +104,12 @@
     onehot[...] = jnp.transpose(jnp.where(ids == assign[...], 1.0, 0.0)).astype(BF16)
     swap = swap_matrix()
 
-    pl.semaphore_wait(barrier, CHIPS + 1 + jnp.where(next_quad, 1, 0))
+    pl.semaphore_wait(barrier, STRIPS + GROUPS - 2)
+    for i in range(1, STRIPS):
+        pl.semaphore_signal(known, inc=1, device_id=g * STRIPS + wrap(s + i, STRIPS), device_id_type=FLAT)
+
+    for i in range(1, 4):
+        remote(part.at[quad], part.at[quad], part_send, part_recv, me - quad + wrap(quad + i, 4)).start()
 
     above, below = jnp.where(s > 0, me - 1, me), jnp.where(s < STRIPS - 1, me + 1, me)
     up_copies = [
@@ -133,9 +130,6 @@
     def _():
         for copy in down_copies:
             copy.start()
-
-    for i in range(1, 4):
-        remote(part.at[quad], part.at[quad], part_send, part_recv, me - quad + wrap(quad + i, 4)).start()
 
     def relayout_weights(i, carry):
         for half in range(2):
@@ -161,6 +155,7 @@
     )
     mine = g * 4 + s // 4
     gath[mine] = tile.astype(BF16)
+    pl.semaphore_wait(known, STRIPS - 1)
 
     for i in range(1, 32):
         remote(gath.at[mine], gath.at[mine], gath_send, gath_recv, wrap(mine + i, 32) * 4 + quad).start()
@@ -304,8 +299,11 @@
         residual_chunk(c)
         back_half(c, 1 - core, False)
 
-    theirs = pl.ds((1 - core) * 64, 64)
-    to_twin = remote(acc.at[theirs], pair_in, pair_send, pair_recv, twin)
+    @pl.loop(0, 8)
+    def _(i):
+        pair_out[pl.ds(i * 8, 8)] = acc[pl.ds((1 - core) * 64 + i * 8, 8)].astype(BF16)
+
+    to_twin = remote(pair_out, pair_in, pair_send, pair_recv, twin)
     to_twin.start()
     back_half(0, core, True)
 
@@ -318,7 +316,7 @@
     @pl.loop(0, 8)
     def _(i):
         at = pl.ds(i * 8, 8)
-        mine_bf[at] = (acc[pl.ds(core * 64 + i * 8, 8)] + pair_in[at]).astype(BF16)
+        mine_bf[at] = (acc[pl.ds(core * 64 + i * 8, 8)] + pair_in[at].astype(F32)).astype(BF16)
 
     each_chip(
         lambda p, device: remote(mine_bf.at[p], pieces.at[chip], piece_send, piece_recv, device).start()
@@ -428,7 +426,7 @@
             pltpu.VMEM((PAIRS, HID, 256), F32),
             pltpu.VMEM((PAIRS, HID, 256), BF16),
             pltpu.VMEM((DEVS, 16, 128), F32),
-            pltpu.VMEM((64, 16, 128), F32),
+            pltpu.VMEM((64, 16, 128), BF16), pltpu.VMEM((64, 16, 128), BF16),
             pltpu.VMEM((CHIPS, 16, 128), BF16), pltpu.VMEM((CHIPS, 16, 128), BF16),
             pltpu.VMEM((DEVS, 16, 128), BF16),
             pltpu.VMEM((DEVS, 16, 128), F32), pltpu.VMEM((HID, HID), BF16),
@@ -437,7 +435,7 @@
             pltpu.VMEM((1, ROWS, 1024), F32), pltpu.VMEM((1, ROWS, 1024), F32), pltpu.VMEM((1, HID), jnp.int32), pltpu.VMEM((4, FEAT), BF16),
             dma((4,)), dma((4,)), dma, dma, dma, dma, dma, dma((4,)),
             dma, dma, dma, dma, dma, dma, dma, dma,
-            dma((3,)), dma((8,)), dma, dma((4,)),
+            dma((3,)), dma((8,)), dma, dma((4,)), pltpu.SemaphoreType.REGULAR,
         ],
         compiler_params=pltpu.CompilerParams(
             collective_id=0, has_side_effects=True, vmem_limit_bytes=MAIN_VMEM

time: 61.3 us -> 58.9 us (0.961)
  Pallas kernels: 59.8 us -> 57.4 us
    pallas_call x1, Pallas kernels: 55.9 us -> 53.5 us  [per_device(): pl.pallas_call(main_kernel, out_shape=(shape((HID, ROWS, 128), BF16),) +...]
where the time goes in v6:
time: 58.9 us; the launch traced here: 58.7 us
  Pallas kernels  57.4 us (97%)
  between operations  1.29 us (2%)
    pallas_call x1, Pallas kernels, per_device(): pl.pallas_call(main_kernel, out_shape=(shape((HID, ROWS, 128), BF16),) +...  53.5 us
    pallas_call x1, Pallas kernels, per_device(): pl.pallas_call(final_kernel, out_shape=(shape((FEAT, HID), F32), shape((H...  3.96 us

profile of v6, /device:TPU:1, one launch (start us, length us, event | category | flops | bytes accessed | tf_op | source)
XLA Modules:
  0.0 58.7 jit_solution(2105258407365011650)
XLA Ops:
  1.3 53.5 %solve_and_reduce.1 = (bf16[512,32,128]{2,1,0:T(8,128)(2,1)S(1)}, f32[512,512]{1,0:T(8,128)S(1)}, f32[512,512]{1,0:T(8,128)S(1)}, bf16[512,512]{1,0:T(8,128)(2,1...) custom-call(f32[1,32,1024]{2,1,0:T(8,128)} %initial_hbm.1, ...), custom_call_target="tpu_custom_call" | custom-call | tf_op jit(solution)/shard_map/solve_and_reduce/pallas_call | solution.py:411
  54.8 4.0 %outputs.1 = (f32[128,512]{1,0:T(8,128)}, f32[512,512]{1,0:T(8,128)}, f32[512,512]{1,0:T(8,128)}, bf16[512,32,128]{2,1,0:T(8,128)(2,1)}) custom-call(bf16[512,32,128]{2,1,0:T(8,128)(2,1)S(1)} %get-tuple-element.11.gout_in, f32[512,512]{1,0:T(8,128)S(1)} %get-tuple-element.12.act_a, f32[512,512]{1,0:T(8,128)S(1)} %get-tuple-element.13.act_b, ...), custom_call_target="tpu_custom_call" | custom-call | tf_op jit(solution)/shard_map/outputs/pallas_call | solution.py:448

commit v7 on v6

--- a/solution.py
+++ b/solution.py
@@ -13,6 +13,9 @@
 REGION = 3 * ROWS
 PAIRS = ROWS // 2
 CHUNK = 4
+OFFSETS = sorted(
+    [(i // 16, i // 4 % 4, i % 4) for i in range(1, 64)], key=lambda o: -sum(min(d, 4 - d) for d in o)
+)
 PAD = 8
 MAIN_VMEM = 42 * 1024 * 1024
 
@@ -52,12 +55,13 @@
     def wrap(i, n):
         return jnp.where(i >= n, i - n, i)
 
+    ring = lambda v, stride: [wrap(v + d, 4) * stride for d in range(4)]
+    ys, xs, zs = ring(chip // 16, 16), ring(chip // 4 % 4, 4), ring(chip % 4, 1)
+
     def each_chip(fn):
-        @pl.loop(0, 7)
-        def _(i):
-            for j in range(9):
-                p = wrap(chip + 1 + i * 9 + j, CHIPS)
-                fn(p, p * 2 + core)
+        for dy, dx, dz in OFFSETS:
+            p = ys[dy] + xs[dx] + zs[dz]
+            fn(p, p * 2 + core)
 
     def remote(src, dst, send_sem, recv_sem, device):
         return pltpu.make_async_remote_copy(

time: 58.9 us -> 58 us (0.985)
  Pallas kernels: 57.4 us -> 56.5 us
    pallas_call x1, Pallas kernels: 53.5 us -> 52.6 us  [per_device(): pl.pallas_call(main_kernel, out_shape=(shape((HID, ROWS, 128), BF16),) +...]
where the time goes in v7:
time: 58 us; the launch traced here: 57.8 us
  Pallas kernels  56.5 us (97%)
  between operations  1.29 us (2%)
    pallas_call x1, Pallas kernels, per_device(): pl.pallas_call(main_kernel, out_shape=(shape((HID, ROWS, 128), BF16),) +...  52.6 us
    pallas_call x1, Pallas kernels, per_device(): pl.pallas_call(final_kernel, out_shape=(shape((FEAT, HID), F32), shape((H...  3.96 us

profile of v7, /device:TPU:1, one launch (start us, length us, event | category | flops | bytes accessed | tf_op | source)
XLA Modules:
  0.0 57.8 jit_solution(7671231125777698269)
XLA Ops:
  1.3 52.6 %solve_and_reduce.1 = (bf16[512,32,128]{2,1,0:T(8,128)(2,1)S(1)}, f32[512,512]{1,0:T(8,128)S(1)}, f32[512,512]{1,0:T(8,128)S(1)}, bf16[512,512]{1,0:T(8,128)(2,1...) custom-call(f32[1,32,1024]{2,1,0:T(8,128)} %initial_hbm.1, ...), custom_call_target="tpu_custom_call" | custom-call | tf_op jit(solution)/shard_map/solve_and_reduce/pallas_call | solution.py:415
  53.9 4.0 %outputs.1 = (f32[128,512]{1,0:T(8,128)}, f32[512,512]{1,0:T(8,128)}, f32[512,512]{1,0:T(8,128)}, bf16[512,32,128]{2,1,0:T(8,128)(2,1)}) custom-call(bf16[512,32,128]{2,1,0:T(8,128)(2,1)S(1)} %get-tuple-element.11.gout_in, f32[512,512]{1,0:T(8,128)S(1)} %get-tuple-element.12.act_a, f32[512,512]{1,0:T(8,128)S(1)} %get-tuple-element.13.act_b, ...), custom_call_target="tpu_custom_call" | custom-call | tf_op jit(solution)/shard_map/outputs/pallas_call | solution.py:452

commit v8 on v7

--- a/solution.py
+++ b/solution.py
@@ -15,6 +15,11 @@
 CHUNK = 4
 OFFSETS = sorted(
     [(i // 16, i // 4 % 4, i % 4) for i in range(1, 64)], key=lambda o: -sum(min(d, 4 - d) for d in o)
+)
+GROUP_OFFSETS = sorted([(i // 2, i % 2) for i in range(1, 8)], key=lambda o: -min(o[0], 4 - o[0]) - 2 * o[1])
+TILE_OFFSETS = sorted(
+    [(i // 8, i // 2 % 4, i % 2) for i in range(1, 32)],
+    key=lambda o: -min(o[0], 4 - o[0]) - min(o[1], 4 - o[1]) - 2 * o[2],
 )
 PAD = 8
 MAIN_VMEM = 42 * 1024 * 1024
@@ -161,8 +166,9 @@
     gath[mine] = tile.astype(BF16)
     pl.semaphore_wait(known, STRIPS - 1)
 
-    for i in range(1, 32):
-        remote(gath.at[mine], gath.at[mine], gath_send, gath_recv, wrap(mine + i, 32) * 4 + quad).start()
+    for dy, dx, dz in TILE_OFFSETS:
+        other = ys[dy] // 2 + xs[dx] // 2 + wrap(mine % 2 + dz, 2)
+        remote(gath.at[mine], gath.at[mine], gath_send, gath_recv, other * 4 + quad).start()
 
     def land(has, copies_in, copies_out, rows):
         @pl.when(has)
@@ -239,8 +245,8 @@
 
     for c in range(PAIRS // CHUNK):
         pack(c)
-        for i in range(1, GROUPS):
-            snap_copy(c, wrap(g + i, GROUPS)).start()
+        for dy, dx in GROUP_OFFSETS:
+            snap_copy(c, wrap(g // 2 + dy, 4) * 2 + wrap(g % 2 + dx, 2)).start()
 
     own = pltpu.make_async_copy(
         send.at[g], snaps.at[:, pl.ds(pl.multiple_of(g * SNAPS, SNAPS), SNAPS), :], own_sem

time: 58 us -> 57.7 us (level)
  no operation moved by 1% of the time
where the time goes in v8:
time: 57.7 us; the launch traced here: 57.6 us
  Pallas kernels  56.3 us (98%)
  between operations  1.29 us (2%)
    pallas_call x1, Pallas kernels, per_device(): pl.pallas_call(main_kernel, out_shape=(shape((HID, ROWS, 128), BF16),) +...  52.3 us
    pallas_call x1, Pallas kernels, per_device(): pl.pallas_call(final_kernel, out_shape=(shape((FEAT, HID), F32), shape((H...  3.96 us

profile of v8, /device:TPU:1, one launch (start us, length us, event | category | flops | bytes accessed | tf_op | source)
XLA Modules:
  0.0 57.6 jit_solution(10936363515229658720)
XLA Ops:
  1.3 52.3 %solve_and_reduce.1 = (bf16[512,32,128]{2,1,0:T(8,128)(2,1)S(1)}, f32[512,512]{1,0:T(8,128)S(1)}, f32[512,512]{1,0:T(8,128)S(1)}, bf16[512,512]{1,0:T(8,128)(2,1...) custom-call(f32[1,32,1024]{2,1,0:T(8,128)} %initial_hbm.1, ...), custom_call_target="tpu_custom_call" | custom-call | tf_op jit(solution)/shard_map/solve_and_reduce/pallas_call | solution.py:421
  53.6 4.0 %outputs.1 = (f32[128,512]{1,0:T(8,128)}, f32[512,512]{1,0:T(8,128)}, f32[512,512]{1,0:T(8,128)}, bf16[512,32,128]{2,1,0:T(8,128)(2,1)}) custom-call(bf16[512,32,128]{2,1,0:T(8,128)(2,1)S(1)} %get-tuple-element.11.gout_in, f32[512,512]{1,0:T(8,128)S(1)} %get-tuple-element.12.act_a, f32[512,512]{1,0:T(8,128)S(1)} %get-tuple-element.13.act_b, ...), custom_call_target="tpu_custom_call" | custom-call | tf_op jit(solution)/shard_map/outputs/pallas_call | solution.py:458

commit v9 on v8

--- a/solution.py
+++ b/solution.py
@@ -274,9 +274,10 @@
         for kb in range(4):
             act_c[pl.ds(kb * 32 + m * 8, 8)] = c[:, kb * 128 : kb * 128 + 128].reshape(8, 16, 128)
 
-    @pl.loop(0, PAIRS)
-    def _(rp):
-        pred[rp] = dot(hidc[...], w2[rp])
+    @pl.loop(0, PAIRS // 2)
+    def _(i):
+        for half in range(2):
+            pred[2 * i + half] = dot(hidc[...], w2[2 * i + half])
 
     own.wait()
     inverse_root = F32(1.0) / jnp.sqrt(F32(HID))

time: 57.7 us -> 57.7 us (level)
  no operation moved by 1% of the time
where the time goes in v9:
time: 57.7 us; the launch traced here: 57.6 us
  Pallas kernels  56.3 us (98%)
  between operations  1.29 us (2%)
    pallas_call x1, Pallas kernels, per_device(): pl.pallas_call(main_kernel, out_shape=(shape((HID, ROWS, 128), BF16),) +...  52.3 us
    pallas_call x1, Pallas kernels, per_device(): pl.pallas_call(final_kernel, out_shape=(shape((FEAT, HID), F32), shape((H...  3.96 us

profile of v9, /device:TPU:1, one launch (start us, length us, event | category | flops | bytes accessed | tf_op | source)
XLA Modules:
  0.0 57.6 jit_solution(12141210790492153178)
XLA Ops:
  1.3 52.3 %solve_and_reduce.1 = (bf16[512,32,128]{2,1,0:T(8,128)(2,1)S(1)}, f32[512,512]{1,0:T(8,128)S(1)}, f32[512,512]{1,0:T(8,128)S(1)}, bf16[512,512]{1,0:T(8,128)(2,1...) custom-call(f32[1,32,1024]{2,1,0:T(8,128)} %initial_hbm.1, ...), custom_call_target="tpu_custom_call" | custom-call | tf_op jit(solution)/shard_map/solve_and_reduce/pallas_call | solution.py:422
  53.6 4.0 %outputs.1 = (f32[128,512]{1,0:T(8,128)}, f32[512,512]{1,0:T(8,128)}, f32[512,512]{1,0:T(8,128)}, bf16[512,32,128]{2,1,0:T(8,128)(2,1)}) custom-call(bf16[512,32,128]{2,1,0:T(8,128)(2,1)S(1)} %get-tuple-element.11.gout_in, f32[512,512]{1,0:T(8,128)S(1)} %get-tuple-element.12.act_a, f32[512,512]{1,0:T(8,128)S(1)} %get-tuple-element.13.act_b, ...), custom_call_target="tpu_custom_call" | custom-call | tf_op jit(solution)/shard_map/outputs/pallas_call | solution.py:459
